TPU v7x, 32 devices: a whole 2x2x4 slice. The times are simulated.
32 devices in a mesh: prow: 4 (over z), pcol: 8 (over y, x, core).
Axes of the slice: x: 2, y: 2, z: 4, core: 2. Of those that a mesh axis runs over, the one named last changes fastest.
Arguments:
- anc_inverse: float32 [2048, 2048], P('pcol', 'prow')
- pattern_one: int32 [8, 4], replicated, may hold values from 0 to 7, as said below
- parents: int32 [8], replicated, may hold values from 0 to 7, as said below
- low_one: float32 [8, 1024, 256], P('pcol', 'prow'), may hold values from -2 to 2
- pivot_one: float32 [8, 256, 256], P('pcol'), may hold values from -4 to 4
- low_two: float32 [8, 1024, 256], P('pcol', 'prow'), may hold values from -2 to 2
- second_scaled_factor: float32 [8, 256, 256], P('pcol'), may hold values from -2 to 2
- second_pivot_inverse: float32 [8, 256, 256], P('pcol'), may hold values from -4 to 4
Outputs:
- column_one: float32 [8, 2048, 256], P('prow', 'pcol')
- diag_one: float32 [8, 256, 256], P('pcol')
- column_two: float32 [8, 2048, 256], P('prow', 'pcol')
- second_parent_inverse: float32 [8, 256, 256], P('pcol')
- second_diagonal_inverse: float32 [8, 256, 256], P('pcol')
Inputs may be any that keep to these rules, and one draw needn't show every extreme that they name: `pattern_one`: entry r of each row names an ancestor of process row r: it lies in r * 2 to r * 2 + 1; for each r, every ancestor of that range is entry r of exactly 4 rows. `parents`: every first-level supernode is the parent of exactly one second-level supernode.
All inputs are finite; a program needn't handle non-finite values.
Results may differ from a plain program's by a relative error of at most 0.000073.
Values sent between devices are 32-bit elements; how exact they have to be, the bound alone decides.
A program may use at most 128 MiB of HBM per device.

v0:
```python
import functools

import jax
import jax.numpy as jnp
from jax import lax
from jax.experimental import pallas as pl
from jax.experimental.pallas import tpu as pltpu
from jax.sharding import PartitionSpec as P

MESH = pl.DeviceIdType.MESH
CORES = 2


def split_dot(left, right, transposed):
    contract = (((0,), (0,)), ((), ())) if transposed else (((1,), (0,)), ((), ()))
    dot = functools.partial(
        lax.dot_general, dimension_numbers=contract, preferred_element_type=jnp.float32
    )
    left_hi, right_hi = left.astype(jnp.bfloat16), right.astype(jnp.bfloat16)
    left_lo = (left - left_hi.astype(jnp.float32)).astype(jnp.bfloat16)
    right_lo = (right - right_hi.astype(jnp.float32)).astype(jnp.bfloat16)
    return dot(left_hi, right_lo) + dot(left_lo, right_hi) + dot(left_hi, right_hi)


def product_kernel(transposed, keep_at, negate, prefetched, *refs):
    left, right, out = refs[prefetched], refs[prefetched + 1], refs[-1]
    value = split_dot(left[0], right[0], transposed)
    if keep_at is not None:
        value = jnp.where(refs[keep_at][pl.program_id(0)] > 0, value, 0.0)
    if len(refs) > prefetched + 3:
        value = refs[prefetched + 2][0] - value
    elif negate:
        value = -value
    out[0] = value


def products(
    count, left, right, left_index=None, right_index=None, transposed=False, keep=None,
    minus_from=None, negate=False,
):
    width = left.shape[1]
    block = (1, width, width)
    prefetch = []

    def chosen(index):
        if index is None:
            return pl.BlockSpec(block, lambda g, *p: (g, 0, 0))
        at = len(prefetch)
        prefetch.append(index.astype(jnp.int32))
        return pl.BlockSpec(block, lambda g, *p: (p[at][g], 0, 0))

    specs = [chosen(left_index), chosen(right_index)]
    args = [left, right]
    if minus_from is not None:
        specs.append(chosen(None))
        args.append(minus_from)
    keep_at = None
    if keep is not None:
        keep_at = len(prefetch)
        prefetch.append(keep.astype(jnp.int32))
    return pl.pallas_call(
        functools.partial(product_kernel, transposed, keep_at, negate, len(prefetch)),
        out_shape=jax.ShapeDtypeStruct((count, width, width), jnp.float32),
        grid_spec=pltpu.PrefetchScalarGridSpec(
            num_scalar_prefetch=len(prefetch),
            grid=(count,),
            in_specs=specs,
            out_specs=chosen(None),
        ),
    )(*prefetch, *args)


def exchange_kernel(kinds, rows, cols, *refs):
    count = len(kinds)
    sources, targets = refs[:count], refs[count : 2 * count]
    sems = refs[2 * count :]
    row, col = lax.axis_index("prow"), lax.axis_index("pcol")
    per = cols // rows
    chips = cols // CORES
    chip, core = col // CORES, lax.rem(col, CORES)
    partner = chip * CORES + (1 - core)
    own_place, home = lax.rem(col, per), col // per
    used = [axis for _, axis in kinds]

    barrier = pltpu.get_barrier_semaphore()
    expected = 0
    if "pcol" in used:
        for d in range(1, cols):
            pl.semaphore_signal(
                barrier, inc=1, device_id=(row, lax.rem(col + d, cols)), device_id_type=MESH
            )
        expected += cols - 1
    if "prow" in used:
        for d in range(1, rows):
            pl.semaphore_signal(
                barrier, inc=1, device_id=(lax.rem(row + d, rows), col), device_id_type=MESH
            )
        expected += rows - 1
    if "both" in used:

        @pl.when(home != row)
        def _():
            pl.semaphore_signal(
                barrier, inc=1, device_id=(home, row * per + own_place), device_id_type=MESH
            )

        expected += jnp.where(home != row, 1, 0)
    pl.semaphore_wait(barrier, expected)

    def remote(source, target, send, recv, device):
        return pltpu.make_async_remote_copy(
            src_ref=source,
            dst_ref=target,
            send_sem=send,
            recv_sem=recv,
            device_id=device,
            device_id_type=MESH,
        )

    copies, forwards, locals_ = [], [], []
    for op, (kind, axis) in enumerate(kinds):
        x, out = sources[op], targets[op]
        send, recv = sems[2 * op], sems[2 * op + 1]
        if kind == "transpose":
            continue
        size, me = (rows, row) if axis == "prow" else (cols, col)
        if kind == "gather" and axis == "pcol":
            for d in range(1, chips):
                there = lax.rem(chip + d, chips) * CORES + core
                copy = remote(x, out.at[me], send.at[d], recv.at[d], (row, there))
                copy.start()
                here = lax.rem(chip + chips - d, chips) * CORES + core
                forwards.append((copy, op, d, here))
            copy = remote(x, out.at[me], send.at[0], recv.at[0], (row, partner))
            copy.start()
            copies.append(copy)
        else:
            for d in range(1, size):
                there = lax.rem(me + d, size)
                device = (there, col) if axis == "prow" else (row, there)
                source = x if kind == "gather" else x.at[there]
                copy = remote(source, out.at[me], send.at[d], recv.at[d], device)
                copy.start()
                copies.append(copy)
        mine = x if kind == "gather" else x.at[me]
        local = pltpu.make_async_copy(mine, out.at[me], sems[2 * count].at[op])
        local.start()
        locals_.append(local)

    def away(op):
        return remote(
            sources[op],
            targets[op].at[own_place],
            sems[2 * op].at[0],
            sems[2 * op + 1].at[0],
            (home, row * per + own_place),
        )

    def near(op):
        return pltpu.make_async_copy(
            sources[op], targets[op].at[own_place], sems[2 * op + 1].at[0]
        )

    transposes = [op for op, (kind, _) in enumerate(kinds) if kind == "transpose"]
    for op in transposes:

        @pl.when(home == row)
        def _():
            near(op).start()

        @pl.when(home != row)
        def _():
            away(op).start()

    for copy, op, d, here in forwards:
        copy.wait_recv()
        out = targets[op]
        forward = remote(
            out.at[here],
            out.at[here],
            sems[2 * op].at[chips - 1 + d],
            sems[2 * op + 1].at[chips - 1 + d],
            (row, partner),
        )
        forward.start()
        copies.append(forward)
    for op in transposes:
        near(op).wait()

        @pl.when(home != row)
        def _():
            away(op).wait_send()

        out = targets[op]
        for d in range(1, per):
            there = home * per + lax.rem(own_place + d, per)
            forward = remote(
                out.at[own_place],
                out.at[own_place],
                sems[2 * op].at[d],
                sems[2 * op + 1].at[d],
                (row, there),
            )
            forward.start()
            copies.append(forward)
    for copy, _, _, _ in forwards:
        copy.wait_send()
    for copy in copies:
        copy.wait_send()
        copy.wait_recv()
    for local in locals_:
        local.wait()
def exchange(number, *ops):
    rows, cols = lax.axis_size("prow"), lax.axis_size("pcol")
    shapes, scratch, kinds = [], [], []
    for kind, axis, x in ops:
        size = {"prow": rows, "pcol": cols, "both": cols // rows}[axis]
        lead = x.shape if kind != "all" else x.shape[1:]
        shapes.append(jax.ShapeDtypeStruct((size,) + lead, x.dtype))
        scratch += [pltpu.SemaphoreType.DMA((size,))] * 2
        kinds.append((kind, axis))
    scratch.append(pltpu.SemaphoreType.DMA((len(ops),)))
    anywhere = pl.BlockSpec(memory_space=pl.ANY)
    return pl.pallas_call(
        functools.partial(exchange_kernel, tuple(kinds), rows, cols),
        out_shape=shapes,
        in_specs=[anywhere] * len(ops),
        out_specs=[anywhere] * len(ops),
        scratch_shapes=scratch,
        compiler_params=pltpu.CompilerParams(collective_id=number, has_side_effects=True),
    )(*[x for _, _, x in ops])


def body(
    anc_inverse,
    pattern_one,
    parents,
    low_one,
    pivot_one,
    low_two,
    second_scaled_factor,
    second_pivot_inverse,
):
    row, col = lax.axis_index("prow"), lax.axis_index("pcol")
    rows, cols = lax.axis_size("prow"), lax.axis_size("pcol")
    per = cols // rows
    width = pivot_one.shape[1]
    piece = width // cols
    owned = anc_inverse.shape[1] // width
    zblocks = anc_inverse.reshape(width, owned, width).transpose(1, 0, 2)
    everyone = jnp.arange(cols, dtype=jnp.int32)
    place = col // per
    child = jnp.zeros((cols,), jnp.int32).at[parents].set(everyone)
    row_slots = lax.dynamic_index_in_dim(pattern_one, row, 1, keepdims=False) - row * owned
    row_slots_two = jnp.take(row_slots, parents)
    place_slots = lax.dynamic_index_in_dim(pattern_one, place, 1, keepdims=False)
    hit_one = lax.dynamic_slice_in_dim(place_slots, row * per, per) == col
    hit_two = lax.dynamic_slice_in_dim(jnp.take(place_slots, parents), row * per, per) == col
    one, two = low_one[0], low_two[0]

    def pieces(blocks):
        return blocks.reshape(per, cols, piece, width).transpose(1, 0, 2, 3)

    lowall, one_t, pivot_pieces = exchange(
        0,
        ("gather", "pcol", one),
        ("transpose", "both", one),
        ("all", "pcol", pivot_one.reshape(cols, piece, width)),
    )
    parent_index = lax.dynamic_slice_in_dim(parents, col, 1)
    merged = products(
        1, lowall, second_scaled_factor, left_index=parent_index, minus_from=low_two
    )[0]
    first_terms = products(cols, zblocks, lowall, left_index=row_slots, negate=True)
    mergedall, first_got, two_t, pivot_parent = exchange(
        1,
        ("gather", "pcol", merged),
        ("all", "prow", first_terms.reshape(rows, per, width, width)),
        ("transpose", "both", two),
        ("all", "pcol", jnp.take(pivot_pieces, parents, axis=0)),
    )
    column_one = jnp.sum(first_got, axis=0)
    pivot_terms = products(per, one_t, column_one, transposed=True, keep=hit_one)
    second_terms = products(
        cols, zblocks, mergedall, left_index=row_slots_two, negate=True
    )
    of_child = lax.dynamic_index_in_dim(
        mergedall, lax.dynamic_index_in_dim(child, col, 0, keepdims=False), 0, keepdims=False
    )
    second_got, child_t, pivot_got = exchange(
        2,
        ("all", "prow", second_terms.reshape(rows, per, width, width)),
        ("transpose", "both", of_child),
        ("all", "pcol", pieces(pivot_terms)),
    )
    column_two = jnp.sum(second_got, axis=0)
    pivot_piece = jnp.sum(pivot_got, axis=0)
    cross_terms = products(per, column_one, child_t, transposed=True, keep=hit_one)
    diag_terms = products(per, two_t, column_two, transposed=True, keep=hit_two)
    small_got, pivot_rows = exchange(
        3,
        ("all", "pcol", jnp.concatenate([pieces(cross_terms), pieces(diag_terms)], axis=1)),
        ("gather", "prow", pivot_piece),
    )
    pivot_rows = pivot_rows.reshape(cols, piece, width)
    small_rows, pivot_final = exchange(
        4,
        ("gather", "prow", jnp.sum(small_got, axis=0)),
        (
            "all",
            "pcol",
            jnp.stack([pivot_rows, jnp.take(pivot_rows, parents, axis=0)], axis=1),
        ),
    )
    cross_rows = small_rows[:, :per].reshape(cols, piece, width)
    diag_rows = small_rows[:, per:].reshape(cols, piece, width)
    (small_final,) = exchange(
        5,
        ("all", "pcol", jnp.stack([jnp.take(cross_rows, parents, axis=0), diag_rows], axis=1)),
    )

    def whole(array, index):
        return array[:, index].reshape(1, width, width)

    diag_one = pivot_one - whole(pivot_final, 0)
    parent_sum = whole(pivot_final, 1)
    left = pivot_parent.reshape(1, width, width) - parent_sum + parent_sum.transpose(0, 2, 1)
    second_parent_inverse = products(
        1, left, second_scaled_factor, minus_from=-whole(small_final, 0)
    )
    second_diagonal_inverse = products(
        1,
        second_scaled_factor,
        second_parent_inverse,
        transposed=True,
        minus_from=second_pivot_inverse - whole(small_final, 1),
    )
    return (column_one, diag_one, column_two, second_parent_inverse, second_diagonal_inverse)


def solution(mesh):
    placed = (
        P("pcol", "prow"),
        P(),
        P(),
        P("pcol", "prow", None),
        P("pcol", None, None),
        P("pcol", "prow", None),
        P("pcol", None, None),
        P("pcol", None, None),
    )
    return jax.shard_map(
        body,
        mesh=mesh,
        in_specs=placed,
        out_specs=(
            P("prow", "pcol", None),
            P("pcol", None, None),
            P("prow", "pcol", None),
            P("pcol", None, None),
            P("pcol", None, None),
        ),
        check_vma=False,
    )
```

profile of v0, /device:TPU:24, one launch (start us, length us, event | category | flops | bytes accessed | tf_op | source)
XLA Modules:
  0.0 263.4 jit_solution(1754620364775697352)
XLA Ops:
  0.7 1.2 dynamic_slice.24.refs_0_
  1.9 1.3 fusion.3.refs_0_
  9.1 1.3 broadcast_select_fusion.2
  10.9 1.2 copy.16
  12.2 1.0 copy.17
  13.2 28.4 %shard_map.119 = (f32[8,256,256]{2,1,0:T(8,128)}, f32[2,256,256]{2,1,0:T(8,128)}, f32[8,32,256]{2,1,0:T(8,128)}) custom-call(f32[256,256]{1,0:T(8,128)} %bitcast.58, f32[256,256]{1,0:T(8,128)} %bitcast.59, f32[8,32,256]{2,1,0:T(8,128)} %bitcast.60), custom_call_target="tpu_custom_call" | custom-call | tf_op jit(solution)/shard_map/pallas_call | solution.py:224
  41.6 1.5 gather_fusion
  43.9 2.7 %shard_map.120 = f32[1,256,256]{2,1,0:T(8,128)} custom-call(s32[1]{0:T(128)} %dynamic_slice.24.refs_0_, f32[8,256,256]{2,1,0:T(8,128)} %get-tuple-element.21.refs_1_.refs_2_, f32[1,256,256]{2,1,0:T(8,128)} %refs_0_.1, f32[1,256,256]{2,1,0:T(8,128)} %refs_3_.1), custom_call_target="tpu_custom_call" | custom-call | tf_op jit(solution)/shard_map/pallas_call | solution.py:61
  46.6 7.6 %shard_map.121 = f32[8,256,256]{2,1,0:T(8,128)} custom-call(s32[8]{0:T(128)} %copy-done, f32[2,256,256]{2,1,0:T(8,128)} %bitcast.49, f32[8,256,256]{2,1,0:T(8,128)} %get-tuple-element.21.refs_1_.refs_2_), custom_call_target="tpu_custom_call" | custom-call | tf_op jit(solution)/shard_map/pallas_call | solution.py:61
  54.3 49.8 %shard_map.122 = (f32[8,256,256]{2,1,0:T(8,128)}, f32[4,2,256,256]{3,2,1,0:T(8,128)}, f32[2,256,256]{2,1,0:T(8,128)}, f32[8,32,256]{2,1,0:T(8,128)}) custom-call(f32[256,256]{1,0:T(8,128)} %bitcast.67, f32[4,2,256,256]{3,2,1,0:T(8,128)} %bitcast.47, f32[256,256]{1,0:T(8,128)} %bitcast.66, f32[8,32,256]{2,1,0:T(8,128)} %broadcast_select_fusion.refs_3_), custom_call_target="tpu_custom_call" | custom-call | tf_op jit(solution)/shard_map/pallas_call | solution.py:224
  104.0 2.6 reduce_sum.36.refs_2_.refs_1_
  106.6 3.1 %shard_map.124 = f32[2,256,256]{2,1,0:T(8,128)} custom-call(s32[2]{0:T(128)} %fusion.3.refs_0_, f32[2,256,256]{2,1,0:T(8,128)} %get-tuple-element.25.refs_1_, f32[2,256,256]{2,1,0:T(8,128)} %reduce_sum.36.refs_2_.refs_1_), custom_call_target="tpu_custom_call" | custom-call | tf_op jit(solution)/shard_map/pallas_call | solution.py:61
  109.7 1.9 copy.25
  111.5 1.7 dynamic-slice_bitcast_fusion.refs_1_
  113.2 7.5 %shard_map.123 = f32[8,256,256]{2,1,0:T(8,128)} custom-call(s32[8]{0:T(128)} %get-tuple-element.35.refs_0_, f32[2,256,256]{2,1,0:T(8,128)} %bitcast.50, f32[8,256,256]{2,1,0:T(8,128)} %get-tuple-element.24.refs_2_), custom_call_target="tpu_custom_call" | custom-call | tf_op jit(solution)/shard_map/pallas_call | solution.py:61
  120.7 62.0 %shard_map.125 = (f32[4,2,256,256]{3,2,1,0:T(8,128)}, f32[2,256,256]{2,1,0:T(8,128)}, f32[8,2,32,256]{3,2,1,0:T(8,128)}) custom-call(f32[4,2,256,256]{3,2,1,0:T(8,128)} %bitcast.48, f32[256,256]{1,0:T(8,128)} %dynamic-slice_bitcast_fusion.refs_1_, f32[8,2,32,256]{3,2,1,0:T(8,128)} %bitcast.56), custom_call_target="tpu_custom_call" | custom-call | tf_op jit(solution)/shard_map/pallas_call | solution.py:224
  182.7 3.2 %shard_map.126 = f32[2,256,256]{2,1,0:T(8,128)} custom-call(s32[2]{0:T(128)} %fusion.3.refs_0_, f32[2,256,256]{2,1,0:T(8,128)} %reduce_sum.36.refs_2_.refs_1_, f32[2,256,256]{2,1,0:T(8,128)} %get-tuple-element.26.refs_2_), custom_call_target="tpu_custom_call" | custom-call | tf_op jit(solution)/shard_map/pallas_call | solution.py:61
  185.9 1.7 reduce_sum.38.refs_1_
  187.6 1.0 reduce_sum.37.refs_2_
  188.6 3.1 %shard_map.127 = f32[2,256,256]{2,1,0:T(8,128)} custom-call(s32[2]{0:T(128)} %compare_convert_fusion.refs_0_, f32[2,256,256]{2,1,0:T(8,128)} %get-tuple-element.27.refs_1_, f32[2,256,256]{2,1,0:T(8,128)} %reduce_sum.37.refs_2_), custom_call_target="tpu_custom_call" | custom-call | tf_op jit(solution)/shard_map/pallas_call | solution.py:61
  191.6 1.1 copy_bitcast_fusion
  192.8 1.1 pad_maximum_fusion.refs_0_
  193.8 28.1 %shard_map.128 = (f32[8,4,32,256]{3,2,1,0:T(8,128)}, f32[4,2,32,256]{3,2,1,0:T(8,128)}) custom-call(f32[8,4,32,256]{3,2,1,0:T(8,128)} %pad_maximum_fusion.refs_0_, f32[2,32,256]{2,1,0:T(8,128)} %reduce_sum.38.refs_1_), custom_call_target="tpu_custom_call" | custom-call | tf_op jit(solution)/shard_map/pallas_call | solution.py:224
  221.9 2.0 reduce_sum.39.refs_0_
  223.9 1.6 gather_fusion.3
  226.4 17.3 %shard_map.129 = (f32[4,4,32,256]{3,2,1,0:T(8,128)}, f32[8,2,32,256]{3,2,1,0:T(8,128)}) custom-call(f32[4,32,256]{2,1,0:T(8,128)} %reduce_sum.39.refs_0_, f32[8,2,32,256]{3,2,1,0:T(8,128)} %pad_maximum_fusion.1.refs_1_), custom_call_target="tpu_custom_call" | custom-call | tf_op jit(solution)/shard_map/pallas_call | solution.py:224
  243.8 1.1 fusion.8
  247.3 0.8 pad_maximum_fusion.2.refs_0_
  248.1 8.5 %shard_map.130 = f32[8,2,32,256]{3,2,1,0:T(8,128)} custom-call(f32[8,2,32,256]{3,2,1,0:T(8,128)} %pad_maximum_fusion.2.refs_0_), custom_call_target="tpu_custom_call" | custom-call | tf_op jit(solution)/shard_map/pallas_call | solution.py:224
  256.6 1.8 fusion.6
  259.1 2.1 shard_map.131.refs_1_
  261.2 2.1 shard_map.132
  (36 shorter events, 9.3 us)
Async XLA Ops:
  4.0 39.1 %copy-start = (s32[8]{0:T(128)}, s32[8]{0:T(128)S(1)}, u32[]{:S(2)}) copy-start(s32[8]{0:T(128)S(1)} %get-tuple-element.44.refs_0_) | copy-start | bytes 100
  182.7 4.9 %copy-start.1 = (f32[4,2,256,256]{3,2,1,0:T(8,128)S(1)}, f32[4,2,256,256]{3,2,1,0:T(8,128)}, u32[]{:S(2)}) copy-start(f32[4,2,256,256]{3,2,1,0:T(8,128)} %get-tuple-element.28) | copy-start | bytes 6291460
  187.6 4.0 %copy-start.2 = (f32[2,256,256]{2,1,0:T(8,128)S(1)}, f32[2,256,256]{2,1,0:T(8,128)}, u32[]{:S(2)}) copy-start(f32[2,256,256]{2,1,0:T(8,128)} %shard_map.126) | copy-start | bytes 1572868
  221.9 3.7 %copy-start.4 = (f32[4,2,32,256]{3,2,1,0:T(8,128)S(1)}, f32[4,2,32,256]{3,2,1,0:T(8,128)}, u32[]{:S(2)}) copy-start(f32[4,2,32,256]{3,2,1,0:T(8,128)} %get-tuple-element.31) | copy-start | bytes 786436
  223.9 21.0 %copy-start.3 = (f32[1,256,256]{2,1,0:T(8,128)S(1)}, f32[1,256,256]{2,1,0:T(8,128)}, u32[]{:S(2)}) copy-start(f32[1,256,256]{2,1,0:T(8,128)} %param.16) | copy-start | bytes 786436
  225.6 20.2 %copy-start.7 = (f32[8,32,256]{2,1,0:T(8,128)S(1)}, f32[8,32,256]{2,1,0:T(8,128)}, u32[]{:S(2)}) copy-start(f32[8,32,256]{2,1,0:T(8,128)} %get-tuple-element.33) | copy-start | bytes 786436
  243.8 2.8 %copy-start.5 = (f32[4,4,32,256]{3,2,1,0:T(8,128)S(1)}, f32[4,4,32,256]{3,2,1,0:T(8,128)}, u32[]{:S(2)}) copy-start(f32[4,4,32,256]{3,2,1,0:T(8,128)} %get-tuple-element.34) | copy-start | bytes 1572868
  246.6 11.8 %copy-start.6 = (f32[1,256,256]{2,1,0:T(8,128)S(1)}, f32[1,256,256]{2,1,0:T(8,128)}, u32[]{:S(2)}) copy-start(f32[1,256,256]{2,1,0:T(8,128)} %param.19) | copy-start | bytes 786436
where the time goes:
time: 266 us; the launch traced here: 263 us
  Pallas kernels  225 us (85%)
  other arithmetic  19.5 us (7%)
  local copies, waits for them, and re-layouts  15.6 us (6%)
  between operations  2.83 us (1%)
    pallas_call x6, Pallas kernels, exchange(): pl.pallas_call(functools.partial(exchange_kernel, tuple(kinds), rows, col...  194 us
    pallas_call x8, Pallas kernels, products(): pl.pallas_call(functools.partial(product_kernel, transposed, keep_at, neg...  31.4 us

commit v1 on v0

v1 whole, which is shorter than its diff:
```python
import functools

import jax
import jax.numpy as jnp
from jax import lax
from jax.experimental import pallas as pl
from jax.experimental.pallas import tpu as pltpu
from jax.sharding import PartitionSpec as P

MESH = pl.DeviceIdType.MESH
CORES = 2
UP, DOWN = 0, 1
LOW_ONE, LOW_TWO, LOW_PARENT = 0, 1, 2
DIAG, CROSS, SECOND = 0, 1, 2
KINDS = 3


def split(x):
    hi = x.astype(jnp.bfloat16)
    return hi, (x - hi.astype(jnp.float32)).astype(jnp.bfloat16)


def dot3(left, right, transposed=False):
    contract = (((0,), (0,)), ((), ())) if transposed else (((1,), (0,)), ((), ()))
    dot = functools.partial(
        lax.dot_general, dimension_numbers=contract, preferred_element_type=jnp.float32
    )
    return dot(left[0], right[1]) + dot(left[1], right[0]) + dot(left[0], right[0])


def fused_kernel(
    rows,
    cols,
    pattern,
    parents,
    anc,
    low_one,
    pivot_one,
    low_two,
    factor,
    pivot_two,
    out_one,
    out_diag,
    out_two,
    out_cross,
    out_second,
    z,
    low,
    whole_factor,
    scattered,
    scattered_pivot,
    scattered_two,
    staged,
    pivot_own,
    pivot_second,
    sums,
    column,
    parent_column,
    product,
    column_two,
    partial,
    partials,
    reduced,
    final,
    load_sem,
    scatter_send,
    scatter_recv,
    factor_send,
    factor_recv,
    swap_send,
    swap_recv,
    low_send,
    low_recv,
    share_send,
    share_recv,
    z_send,
    z_recv,
    near_send,
    near_recv,
    column_send,
    column_recv,
    column_store,
    part_send,
    part_recv,
    line_send,
    line_recv,
    last_send,
    last_recv,
):
    row, col = lax.axis_index("prow"), lax.axis_index("pcol")
    chips = cols // CORES
    width = factor.shape[1]
    piece = width // chips
    owned = anc.shape[1] // width
    chip, core = col // CORES, lax.rem(col, CORES)
    other = 1 - core
    mine = row * CORES + core
    partner = (row, chip * CORES + other)

    def beside(p):
        return (row, p * CORES + core)

    def turn(start, d, size):
        return lax.rem(start + d + size, size)

    def rows_of(p):
        return pl.ds(pl.multiple_of(p * piece, piece), piece)

    def remote(source, target, send, recv, device):
        return pltpu.make_async_remote_copy(
            src_ref=source,
            dst_ref=target,
            send_sem=send,
            recv_sem=recv,
            device_id=device,
            device_id_type=MESH,
        )

    def order(t):
        below, above = row, rows - 1 - row
        both = 2 * jnp.minimum(below, above)
        paired = t <= both
        distance = jnp.where(paired, (t + 1) // 2, t - both // 2)
        up = jnp.where(paired, lax.rem(t, 2) == 1, above > below)
        return jnp.where(up, row + distance, row - distance)

    sent = []

    loads = [
        pltpu.make_async_copy(
            anc.at[:, pl.ds(b * width, width)], z.at[row, core, b], load_sem.at[b]
        )
        for b in range(owned)
    ]
    loads_low = [
        pltpu.make_async_copy(
            low_one.at[0, rows_of(chip)], scattered.at[core, chip], load_sem.at[owned]
        ),
        pltpu.make_async_copy(
            low_two.at[0, rows_of(chip)], scattered_two.at[chip], load_sem.at[owned + 1]
        ),
        pltpu.make_async_copy(
            pivot_one.at[0, rows_of(chip)], scattered_pivot.at[core, chip], load_sem.at[owned + 2]
        ),
    ]
    loads_last = [
        pltpu.make_async_copy(pivot_one.at[0], pivot_own, load_sem.at[owned + 3]),
        pltpu.make_async_copy(pivot_two.at[0], pivot_second, load_sem.at[owned + 4]),
    ]
    load_factor = pltpu.make_async_copy(factor.at[0], whole_factor, load_sem.at[owned + 5])
    for copy in loads + loads_low + loads_last:
        copy.start()

    @pl.when(chip == row)
    def _():
        load_factor.start()

    barrier = pltpu.get_barrier_semaphore()
    peers = [(turn(row, d, rows), col) for d in range(1, rows)]
    peers += [beside(turn(chip, d, chips)) for d in range(1, chips)] + [partner]
    for device in peers:
        pl.semaphore_signal(barrier, inc=1, device_id=device, device_id_type=MESH)
    pl.semaphore_wait(barrier, len(peers))

    def scatter(op, d, source, target, device):
        return remote(source, target, scatter_send.at[op, d], scatter_recv.at[op, d], device)

    scatters = [
        (low_one, scattered.at[core]),
        (low_two, scattered_two),
        (pivot_one, scattered_pivot.at[core]),
    ]
    swapped = [scattered, scattered_pivot]
    for op, (source, target) in enumerate(scatters):
        for d in range(1, chips):
            p = turn(chip, d, chips)
            copy = scatter(op, d, source.at[0, rows_of(p)], target.at[chip], beside(p))
            copy.start()
            sent.append(copy)

    def z_line(source, direction):
        there = row + 1 if direction == UP else row - 1
        return remote(
            z.at[source, core],
            z.at[source, core],
            z_send.at[direction, source],
            z_recv.at[source],
            (there, col),
        )

    def z_near(source):
        return remote(
            z.at[source, core],
            z.at[source, core],
            near_send.at[source],
            near_recv.at[source],
            partner,
        )

    def z_near_arrival(source):
        return remote(
            z.at[source, other],
            z.at[source, other],
            near_send.at[source],
            near_recv.at[source],
            partner,
        )

    for copy in loads:
        copy.wait()

    @pl.when(row + 1 < rows)
    def _():
        z_line(row, UP).start()

    @pl.when(row > 0)
    def _():
        z_line(row, DOWN).start()

    z_near(row).start()

    def factor_piece(d, part, p):
        return remote(
            whole_factor.at[rows_of(part)],
            whole_factor.at[rows_of(part)],
            factor_send.at[0, d],
            factor_recv.at[0, d],
            beside(p),
        )

    def factor_first(d, p):
        return remote(
            factor.at[0, rows_of(p)],
            whole_factor.at[rows_of(p)],
            factor_send.at[1, d],
            factor_recv.at[1, 0],
            beside(p),
        )

    @pl.when(chip == row)
    def _():
        load_factor.wait()
        for d in range(1, chips):
            p = turn(chip, d, chips)
            factor_first(d, p).start()
            factor_piece(d, chip, p).start()

    def arrivals(op, target):
        for d in range(1, chips):
            p = turn(chip, -d, chips)
            scatter(op, d, target.at[p], target.at[p], beside(p)).wait_recv()

    def swap(op):
        return remote(
            swapped[op].at[core],
            swapped[op].at[core],
            swap_send.at[op],
            swap_recv.at[op],
            partner,
        )

    def swap_arrival(op):
        return remote(
            swapped[op].at[other],
            swapped[op].at[other],
            swap_send.at[op],
            swap_recv.at[op],
            partner,
        )

    for copy in loads_low:
        copy.wait()
    arrivals(0, scatters[0][1])
    swap(0).start()
    sent.append(swap(0))
    arrivals(1, scattered_two)
    swap_arrival(0).wait_recv()
    for plane in range(rows):
        parent = parents[plane * CORES + core]
        staged[plane] = scattered[lax.rem(parent, CORES), parent // CORES]

    def pieces_for(plane):
        return [scattered.at[core, plane], scattered_two.at[plane], staged.at[plane]]

    for e in range(1, rows):
        plane = turn(row, e, rows)
        for kind, source in enumerate(pieces_for(plane)):
            copy = remote(
                source,
                low.at[row, kind, rows_of(chip)],
                low_send.at[kind, e],
                low_recv.at[kind, e],
                (plane, col),
            )
            copy.start()
            sent.append(copy)

    def own_share(kind, d, source):
        return remote(
            source,
            low.at[row, kind, rows_of(chip)],
            share_send.at[rows + kind, d],
            share_recv.at[0, d],
            beside(turn(chip, d, chips)),
        )

    for kind, source in enumerate(pieces_for(row)):
        for d in range(1, chips):
            copy = own_share(kind, d, source)
            copy.start()
            sent.append(copy)
    low[row, LOW_ONE, rows_of(chip)] = scattered[core, row]
    low[row, LOW_TWO, rows_of(chip)] = scattered_two[row]
    low[row, LOW_PARENT, rows_of(chip)] = staged[row]

    def share(e, d, p, part):
        source = turn(row, -e, rows)
        return remote(
            low.at[source, :, rows_of(part)],
            low.at[source, :, rows_of(part)],
            share_send.at[e, d],
            share_recv.at[e, d],
            beside(p),
        )

    @pl.when(chip != row)
    def _():
        factor_first(0, chip).wait_recv()
        for d in range(1, chips):
            p = turn(chip, d, chips)

            @pl.when(p != row)
            def _():
                factor_piece(d, chip, p).start()

    for e in range(1, rows):
        source = turn(row, -e, rows)
        for kind in range(KINDS):
            target = low.at[source, kind, rows_of(chip)]
            remote(
                target, target, low_send.at[kind, e], low_recv.at[kind, e], (source, col)
            ).wait_recv()
        for d in range(1, chips):
            copy = share(e, d, turn(chip, d, chips), chip)
            copy.start()
            sent.append(copy)
    arrivals(2, scatters[2][1])
    swap(1).start()
    sent.append(swap(1))

    parent = parents[mine]

    def chosen(source, at):
        value = z[source, :, 0]
        for b in range(1, owned):
            value = jnp.where(at == b, z[source, :, b], value)
        return value.reshape(CORES * width, width)

    def step(t, carry):
        source = order(t)

        @pl.when(source != row)
        def _():
            z_line(source, UP).wait_recv()

            @pl.when(jnp.logical_and(source < row, row + 1 < rows))
            def _():
                z_line(source, UP).start()

            @pl.when(jnp.logical_and(source > row, row > 0))
            def _():
                z_line(source, DOWN).start()

            z_near(source).start()

        e = lax.rem(row - source + rows, rows)
        for d in range(1, chips):
            p = turn(chip, -d, chips)
            share_arrival = remote(
                low.at[source, :, rows_of(p)],
                low.at[source, :, rows_of(p)],
                share_send.at[0, d],
                share_recv.at[e, d],
                beside(p),
            )
            share_arrival.wait_recv()
        z_near_arrival(source).wait_recv()
        at_one = lax.rem(pattern[mine, source], owned)
        at_two = lax.rem(pattern[parent, source], owned)
        rhs = split(low[source, LOW_ONE])
        lhs = split(chosen(source, at_one))
        first = dot3(lhs, rhs)
        lhs = split(chosen(source, at_two))
        second = dot3(lhs, split(low[source, LOW_PARENT]))
        third = dot3(lhs, split(low[source, LOW_TWO]))

        @pl.when(t == 0)
        def _():
            sums[0] = first
            sums[1] = second
            sums[2] = third

        @pl.when(t > 0)
        def _():
            sums[0] += first
            sums[1] += second
            sums[2] += third

        return carry

    lax.fori_loop(0, rows, step, 0)

    def store_column(at, buffer, out):
        keep = pltpu.make_async_copy(buffer.at[core], out.at[core], column_store.at[at])
        away = remote(
            buffer.at[other], out.at[core], column_send.at[at], column_recv.at[at], partner
        )
        keep.start()
        away.start()
        return keep, away

    def reduce_scatter(kind):
        for d in range(1, chips):
            p = turn(chip, d, chips)
            copy = remote(
                partial.at[kind, rows_of(p)],
                partials.at[kind, chip],
                part_send.at[kind, d],
                part_recv.at[kind, d],
                beside(p),
            )
            copy.start()
            sent.append(copy)

    slot_one = lax.rem(pattern[mine, chip], owned)
    slot_two = lax.rem(pattern[parent, chip], owned)
    column[...] = -sums[0].reshape(CORES, width, width)
    partial[DIAG] = dot3(
        split(low[chip, LOW_ONE]), split(column[slot_one]), transposed=True
    )
    stores = [store_column(0, column, out_one)]
    reduce_scatter(DIAG)

    @pl.when(chip != row)
    def _():
        for d in range(1, chips):
            factor_piece(d, turn(chip, -d, chips), partner[1]).wait_recv()

    swap_arrival(1).wait_recv()
    whole = split(whole_factor[...])
    parent_column[...] = -sums[1].reshape(CORES, width, width)
    scaled = dot3(split(-sums[1]), whole)
    product[...] = scaled.reshape(CORES, width, width)
    column_two[...] = -(scaled + sums[2]).reshape(CORES, width, width)
    two_split = split(low[chip, LOW_TWO])
    cross = dot3(split(low[chip, LOW_PARENT]), split(product[slot_two]), transposed=True)
    cross = cross - dot3(split(parent_column[slot_two]), two_split, transposed=True)
    partial[CROSS] = cross
    pivot_rows = scattered_pivot[lax.rem(parent, CORES), parent // CORES]
    partial[CROSS, rows_of(chip)] -= dot3(split(pivot_rows), whole)
    stores.append(store_column(1, column_two, out_two))
    reduce_scatter(CROSS)
    partial[SECOND] = dot3(two_split, split(column_two[slot_two]), transposed=True) + dot3(
        whole, split(partial[CROSS]), transposed=True
    )
    reduce_scatter(SECOND)

    def line(kind, source, direction):
        there = row + 1 if direction == UP else row - 1
        return remote(
            reduced.at[source, kind],
            reduced.at[source, kind],
            line_send.at[direction, kind, source],
            line_recv.at[kind, source],
            (there, col),
        )

    def last(kind, source):
        d = lax.rem(source - chip + chips, chips)
        return remote(
            reduced.at[source, kind],
            final.at[kind, rows_of(chip)],
            last_send.at[kind, source],
            last_recv.at[kind, d],
            beside(source),
        )

    def hand_on(kind, source):
        @pl.when(source != chip)
        def _():
            last(kind, source).start()

        @pl.when(source == chip)
        def _():
            final[kind, rows_of(chip)] = reduced[source, kind]

    def pass_on(kind, source):
        @pl.when(jnp.logical_and(source <= row, row + 1 < rows))
        def _():
            line(kind, source, UP).start()

        @pl.when(jnp.logical_and(source >= row, row > 0))
        def _():
            line(kind, source, DOWN).start()

    for kind in range(KINDS):
        total = partial[kind, rows_of(chip)]
        for d in range(1, chips):
            p = turn(chip, -d, chips)
            target = partials.at[kind, p]
            remote(
                target, target, part_send.at[kind, d], part_recv.at[kind, d], beside(p)
            ).wait_recv()
            total += partials[kind, p]
        reduced[row, kind] = total
        pass_on(kind, row)
        hand_on(kind, row)

    def spread(n, carry):
        t, kind = 1 + n // KINDS, lax.rem(n, KINDS)
        source = order(t)
        line(kind, source, UP).wait_recv()
        pass_on(kind, source)
        hand_on(kind, source)
        return carry

    lax.fori_loop(0, (rows - 1) * KINDS, spread, 0)

    for copy in loads_last:
        copy.wait()

    def take(kind):
        for d in range(1, chips):
            p = turn(chip, -d, chips)
            target = final.at[kind, rows_of(p)]
            remote(
                target, target, last_send.at[kind, 0], last_recv.at[kind, d], beside(p)
            ).wait_recv()

    take(DIAG)
    out_diag[0] = pivot_own[...] - final[DIAG]
    take(CROSS)
    out_cross[0] = final[CROSS]
    take(SECOND)
    out_second[0] = pivot_second[...] - final[SECOND]

    for keep, away in stores:
        keep.wait()
        away.wait_send()
        away.wait_recv()
    for copy in sent:
        copy.wait_send()

    @pl.when(chip == row)
    def _():
        for d in range(1, chips):
            p = turn(chip, d, chips)
            factor_first(d, p).wait_send()
            factor_piece(d, chip, p).wait_send()

    @pl.when(chip != row)
    def _():
        for d in range(1, chips):
            p = turn(chip, d, chips)

            @pl.when(p != row)
            def _():
                factor_piece(d, chip, p).wait_send()

    def drain(source, carry):
        z_near(source).wait_send()

        @pl.when(jnp.logical_and(source <= row, row + 1 < rows))
        def _():
            z_line(source, UP).wait_send()
            for kind in range(KINDS):
                line(kind, source, UP).wait_send()

        @pl.when(jnp.logical_and(source >= row, row > 0))
        def _():
            z_line(source, DOWN).wait_send()
            for kind in range(KINDS):
                line(kind, source, DOWN).wait_send()

        @pl.when(source != chip)
        def _():
            for kind in range(KINDS):
                last(kind, source).wait_send()

        return carry

    lax.fori_loop(0, rows, drain, 0)


def body(
    anc_inverse,
    pattern_one,
    parents,
    low_one,
    pivot_one,
    low_two,
    second_scaled_factor,
    second_pivot_inverse,
):
    rows, cols = lax.axis_size("prow"), lax.axis_size("pcol")
    width = pivot_one.shape[1]
    chips = cols // CORES
    owned = anc_inverse.shape[1] // width
    piece = width // chips
    if rows != chips:
        raise ValueError("mesh shape")
    smem = pl.BlockSpec(memory_space=pltpu.SMEM)
    anywhere = pl.BlockSpec(memory_space=pl.ANY)
    vmem = pl.BlockSpec(memory_space=pltpu.VMEM)

    def f32(*shape):
        return jax.ShapeDtypeStruct(shape, jnp.float32)

    def buffer(*shape):
        return pltpu.VMEM(shape, jnp.float32)

    dma = pltpu.SemaphoreType.DMA
    block = (width, width)
    return tuple(
        pl.pallas_call(
            functools.partial(fused_kernel, rows, cols),
            out_shape=[
                f32(CORES, *block),
                f32(1, *block),
                f32(CORES, *block),
                f32(1, *block),
                f32(1, *block),
            ],
            in_specs=[smem, smem] + [anywhere] * 6,
            out_specs=[anywhere, vmem, anywhere, vmem, vmem],
            scratch_shapes=[
                buffer(rows, CORES, owned, *block),
                buffer(rows, KINDS, *block),
                buffer(*block),
                buffer(CORES, chips, piece, width),
                buffer(CORES, chips, piece, width),
                buffer(chips, piece, width),
                buffer(rows, piece, width),
                buffer(*block),
                buffer(*block),
                buffer(KINDS, CORES * width, width),
                buffer(CORES, *block),
                buffer(CORES, *block),
                buffer(CORES, *block),
                buffer(CORES, *block),
                buffer(KINDS, *block),
                buffer(KINDS, chips, piece, width),
                buffer(rows, KINDS, piece, width),
                buffer(KINDS, *block),
                dma((owned + 6,)),
                dma((3, chips)),
                dma((3, chips)),
                dma((2, chips)),
                dma((2, chips)),
                dma((2,)),
                dma((2,)),
                dma((KINDS, rows)),
                dma((KINDS, rows)),
                dma((rows + KINDS, chips)),
                dma((rows, chips)),
                dma((2, rows)),
                dma((rows,)),
                dma((rows,)),
                dma((rows,)),
                dma((2,)),
                dma((2,)),
                dma((2,)),
                dma((KINDS, chips)),
                dma((KINDS, chips)),
                dma((2, KINDS, rows)),
                dma((KINDS, rows)),
                dma((KINDS, rows)),
                dma((KINDS, chips)),
            ],
            compiler_params=pltpu.CompilerParams(collective_id=0, has_side_effects=True),
        )(
            pattern_one,
            parents,
            anc_inverse,
            low_one,
            pivot_one,
            low_two,
            second_scaled_factor,
            second_pivot_inverse,
        )
    )


def solution(mesh):
    placed = (
        P("pcol", "prow"),
        P(),
        P(),
        P("pcol", "prow", None),
        P("pcol", None, None),
        P("pcol", "prow", None),
        P("pcol", None, None),
        P("pcol", None, None),
    )
    return jax.shard_map(
        body,
        mesh=mesh,
        in_specs=placed,
        out_specs=(
            P("prow", "pcol", None),
            P("pcol", None, None),
            P("prow", "pcol", None),
            P("pcol", None, None),
            P("pcol", None, None),
        ),
        check_vma=False,
    )
```

time: 266 us -> 120 us (0.45); the launches traced: 263 us -> 120 us
  Pallas kernels: 225 us -> 113 us
  other arithmetic: 19.5 us -> 0 us
  local copies, waits for them, and re-layouts: 15.6 us -> 6.84 us
    pallas_call x14 -> x1, Pallas kernels: 225 us -> 113 us  [body(): pl.pallas_call(functools.partial(fused_kernel, rows, cols), out_shape=[f3...]
    reduce_sum x4 -> x0, other arithmetic: 7.24 us -> none  [the longest x1 2.58 us: body(): column_one = jnp.sum(first_got, axis=0)]
    unnamed x17 -> x14, local copies, waits for them, and re-layouts: 1.27 us -> 6.84 us
    gather x5 -> x0, local copies, waits for them, and re-layouts: 4.92 us -> none  [the longest x1 1.55 us: body(): jnp.take(pivot_rows, parents, axis=0)]
    reshape x2 -> x0, local copies, waits for them, and re-layouts: 2.89 us -> none  [the longest x1 1.89 us: pieces(): return blocks.reshape(per, cols, piece, width).transpose(1, 0, 2, 3)]
    select_n x4 -> x0, other arithmetic: 2.71 us -> none  [the longest x2 1.45 us: body(): jnp.take(pivot_pieces, parents, axis=0)]
where the time goes in v1:
time: 120 us
  Pallas kernels  113 us (94%)
  local copies, waits for them, and re-layouts  6.84 us (6%)
    pallas_call x1, Pallas kernels, body(): pl.pallas_call(functools.partial(fused_kernel, rows, cols), out_shape=[f3...  113 us
    unnamed x14, local copies, waits for them, and re-layouts  6.84 us

profile of v1, /device:TPU:24, one launch (start us, length us, event | category | flops | bytes accessed | tf_op | source)
XLA Modules:
  0.0 120.1 jit_solution(4615425802475264391)
XLA Ops:
  0.6 1.3 %copy.13.pattern = s32[8,4]{1,0:T(8,128)} copy(s32[8,4]{0,1:T(4,128)} %param.9) | data formatting | bytes 256 | tf_op args[1]
  2.0 112.6 %shard_map.119 = (f32[2,256,256]{2,1,0:T(8,128)}, f32[1,256,256]{2,1,0:T(8,128)}, f32[2,256,256]{2,1,0:T(8,128)}, f32[1,256,256]{2,1,0:T(8,128)}, f32[1,256,256]{2,1,0:T(8,128)}) custom-call(s32[8,4]{1,0:T(8,128)} %copy.13.pattern, s32[8]{0:T(128)} %parents.1, f32[256,512]{1,0:T(8,128)} %anc.1, f32[1,256,256]{2,1,0:T(8,128)} %low_one.1, ...), custom_call_target="tpu_custom_call" | custom-call | tf_op jit(solution)/shard_map/pallas_call | solution.py:625
  114.6 0.0 copy-start.3
  114.6 0.0 copy-start
  114.6 1.9 %copy.19 = f32[2,256,256]{2,1,0:T(8,128)} copy(f32[2,256,256]{2,1,0:T(8,128)} %get-tuple-element.10) | data formatting | bytes 1048576
  116.5 0.0 copy-done.3
  116.5 0.7 copy.20
  117.2 0.0 copy-done
  117.2 0.0 copy-start.2
  117.2 0.8 copy.21
  118.0 0.3 copy-done.2
  118.3 0.0 copy-start.1
  118.3 0.7 copy.22
  119.0 0.3 copy-done.1
  119.4 0.7 copy.23
Async XLA Ops:
  114.6 2.0 %copy-start.3 = (f32[1,256,256]{2,1,0:T(8,128)S(1)}, f32[1,256,256]{2,1,0:T(8,128)}, u32[]{:S(2)}) copy-start(f32[1,256,256]{2,1,0:T(8,128)} %get-tuple-element.11) | copy-start | bytes 786436
  114.6 2.7 %copy-start = (f32[2,256,256]{2,1,0:T(8,128)S(1)}, f32[2,256,256]{2,1,0:T(8,128)}, u32[]{:S(2)}) copy-start(f32[2,256,256]{2,1,0:T(8,128)} %get-tuple-element.12) | copy-start | bytes 1572868
  117.2 1.1 copy-start.2
  118.3 1.0 copy-start.1

commit v2 on v1

--- a/solution.py
+++ b/solution.py
@@ -178,46 +178,47 @@
             copy.start()
             sent.append(copy)
 
-    def z_line(source, direction):
+    def z_line(source, b, direction):
         there = row + 1 if direction == UP else row - 1
         return remote(
-            z.at[source, core],
-            z.at[source, core],
-            z_send.at[direction, source],
-            z_recv.at[source],
+            z.at[source, core, b],
+            z.at[source, core, b],
+            z_send.at[direction, source, b],
+            z_recv.at[source, b],
             (there, col),
         )
 
-    def z_near(source):
-        return remote(
-            z.at[source, core],
-            z.at[source, core],
-            near_send.at[source],
-            near_recv.at[source],
+    def z_near(source, b):
+        return remote(
+            z.at[source, core, b],
+            z.at[source, core, b],
+            near_send.at[source, b],
+            near_recv.at[source, b],
             partner,
         )
 
-    def z_near_arrival(source):
-        return remote(
-            z.at[source, other],
-            z.at[source, other],
-            near_send.at[source],
-            near_recv.at[source],
-            partner,
-        )
-
-    for copy in loads:
+    def z_near_arrival(source, b):
+        target = z.at[source, other, b]
+        return remote(target, target, near_send.at[source, b], near_recv.at[source, b], partner)
+
+    def z_pass_on(source, b):
+        @pl.when(jnp.logical_and(source <= row, row + 1 < rows))
+        def _():
+            z_line(source, b, UP).start()
+
+        @pl.when(jnp.logical_and(source >= row, row > 0))
+        def _():
+            z_line(source, b, DOWN).start()
+
+        z_near(source, b).start()
+
+    def z_arrive(source, b):
+        z_line(source, b, UP).wait_recv()
+        z_pass_on(source, b)
+
+    for b, copy in enumerate(loads):
         copy.wait()
-
-    @pl.when(row + 1 < rows)
-    def _():
-        z_line(row, UP).start()
-
-    @pl.when(row > 0)
-    def _():
-        z_line(row, DOWN).start()
-
-    z_near(row).start()
+        z_pass_on(row, b)
 
     def factor_piece(d, part, p):
         return remote(
@@ -295,59 +296,74 @@
             copy.start()
             sent.append(copy)
 
-    def own_share(kind, d, source):
+    masks = [1 << n for n in range((chips - 1).bit_length())]
+    trees = [masks, masks[::-1]]
+    offsets = sorted(range(1, chips), key=lambda o: o.bit_count())
+
+    def flip(p, offset):
+        for mask in masks:
+            if offset & mask:
+                p = p + mask - 2 * mask * lax.rem(p // mask, 2)
+        return p
+
+    def half_of(p, half):
+        size = piece // 2
+        return pl.ds(pl.multiple_of(p * piece + half * size, size), size)
+
+    def share(source, offset, at, part, to, half):
+        e = lax.rem(row - source + rows, rows)
+        target = low.at[source, :, part]
+        return remote(
+            target, target, share_send.at[e, offset, at], share_recv.at[e, to, half], beside(flip(chip, offset))
+        )
+
+    def own_share(kind, source, mask):
         return remote(
             source,
             low.at[row, kind, rows_of(chip)],
-            share_send.at[rows + kind, d],
-            share_recv.at[0, d],
-            beside(turn(chip, d, chips)),
-        )
+            share_send.at[rows + kind, mask, 0],
+            share_recv.at[0, mask, 0],
+            beside(flip(chip, mask)),
+        )
+
+    def share_arrive(source):
+        for offset in offsets:
+            origin = flip(chip, offset)
+            direct = offset in masks
+            if direct:
+                share(source, offset, 0, rows_of(origin), offset, 0).wait_recv()
+            for half, tree in enumerate(trees):
+                if not direct:
+                    share(source, offset, 0, half_of(origin, half), offset, half).wait_recv()
+                came = max(n for n, mask in enumerate(tree) if offset & mask)
+                for mask in tree[came + 1 :]:
+                    copy = share(
+                        source, mask, 2 * offset + half, half_of(origin, half), offset ^ mask, half
+                    )
+                    copy.start()
+                    sent.append(copy)
+
+    def low_arrive(source):
+        e = lax.rem(row - source + rows, rows)
+        for kind in range(KINDS):
+            target = low.at[source, kind, rows_of(chip)]
+            remote(
+                target, target, low_send.at[kind, e], low_recv.at[kind, e], (source, col)
+            ).wait_recv()
+        for mask in masks:
+            copy = share(source, mask, 0, rows_of(chip), mask, 0)
+            copy.start()
+            sent.append(copy)
 
     for kind, source in enumerate(pieces_for(row)):
-        for d in range(1, chips):
-            copy = own_share(kind, d, source)
+        for mask in masks:
+            copy = own_share(kind, source, mask)
             copy.start()
             sent.append(copy)
     low[row, LOW_ONE, rows_of(chip)] = scattered[core, row]
     low[row, LOW_TWO, rows_of(chip)] = scattered_two[row]
     low[row, LOW_PARENT, rows_of(chip)] = staged[row]
 
-    def share(e, d, p, part):
-        source = turn(row, -e, rows)
-        return remote(
-            low.at[source, :, rows_of(part)],
-            low.at[source, :, rows_of(part)],
-            share_send.at[e, d],
-            share_recv.at[e, d],
-            beside(p),
-        )
-
-    @pl.when(chip != row)
-    def _():
-        factor_first(0, chip).wait_recv()
-        for d in range(1, chips):
-            p = turn(chip, d, chips)
-
-            @pl.when(p != row)
-            def _():
-                factor_piece(d, chip, p).start()
-
-    for e in range(1, rows):
-        source = turn(row, -e, rows)
-        for kind in range(KINDS):
-            target = low.at[source, kind, rows_of(chip)]
-            remote(
-                target, target, low_send.at[kind, e], low_recv.at[kind, e], (source, col)
-            ).wait_recv()
-        for d in range(1, chips):
-            copy = share(e, d, turn(chip, d, chips), chip)
-            copy.start()
-            sent.append(copy)
-    arrivals(2, scatters[2][1])
-    swap(1).start()
-    sent.append(swap(1))
-
     parent = parents[mine]
 
     def chosen(source, at):
@@ -356,35 +372,9 @@
             value = jnp.where(at == b, z[source, :, b], value)
         return value.reshape(CORES * width, width)
 
-    def step(t, carry):
-        source = order(t)
-
-        @pl.when(source != row)
-        def _():
-            z_line(source, UP).wait_recv()
-
-            @pl.when(jnp.logical_and(source < row, row + 1 < rows))
-            def _():
-                z_line(source, UP).start()
-
-            @pl.when(jnp.logical_and(source > row, row > 0))
-            def _():
-                z_line(source, DOWN).start()
-
-            z_near(source).start()
-
-        e = lax.rem(row - source + rows, rows)
-        for d in range(1, chips):
-            p = turn(chip, -d, chips)
-            share_arrival = remote(
-                low.at[source, :, rows_of(p)],
-                low.at[source, :, rows_of(p)],
-                share_send.at[0, d],
-                share_recv.at[e, d],
-                beside(p),
-            )
-            share_arrival.wait_recv()
-        z_near_arrival(source).wait_recv()
+    def add_products(source, first_time):
+        for b in range(owned):
+            z_near_arrival(source, b).wait_recv()
         at_one = lax.rem(pattern[mine, source], owned)
         at_two = lax.rem(pattern[parent, source], owned)
         rhs = split(low[source, LOW_ONE])
@@ -393,22 +383,74 @@
         lhs = split(chosen(source, at_two))
         second = dot3(lhs, split(low[source, LOW_PARENT]))
         third = dot3(lhs, split(low[source, LOW_TWO]))
-
-        @pl.when(t == 0)
-        def _():
-            sums[0] = first
-            sums[1] = second
-            sums[2] = third
-
-        @pl.when(t > 0)
-        def _():
-            sums[0] += first
-            sums[1] += second
-            sums[2] += third
-
-        return carry
-
-    lax.fori_loop(0, rows, step, 0)
+        for n, value in enumerate([first, second, third]):
+            sums[n] = value if first_time else sums[n] + value
+
+    sources = [order(t) for t in range(rows)]
+    inner = jnp.logical_and(row > 0, row + 1 < rows)
+
+    @pl.when(inner)
+    def _():
+        for b in range(owned):
+            for source in sources[1:3]:
+                z_arrive(source, b)
+
+    @pl.when(jnp.logical_not(inner))
+    def _():
+        for b in range(owned):
+            z_arrive(sources[1], b)
+
+    share_arrive(row)
+    @pl.when(chip != row)
+    def _():
+        factor_first(0, chip).wait_recv()
+        for d in range(1, chips):
+            p = turn(chip, d, chips)
+
+            @pl.when(p != row)
+            def _():
+                factor_piece(d, chip, p).start()
+
+    arrivals(2, scatters[2][1])
+    swap(1).start()
+    sent.append(swap(1))
+    low_arrive(sources[1])
+
+    @pl.when(jnp.logical_not(inner))
+    def _():
+        for b in range(owned):
+            z_arrive(sources[2], b)
+
+    low_arrive(sources[2])
+    add_products(row, True)
+    for source in sources[3:]:
+        low_arrive(source)
+
+    @pl.when(inner)
+    def _():
+        for source in sources[3:]:
+            z_arrive(source, 0)
+
+    share_arrive(sources[1])
+    share_arrive(sources[2])
+
+    @pl.when(inner)
+    def _():
+        for source in sources[3:]:
+            for b in range(1, owned):
+                z_arrive(source, b)
+
+    add_products(sources[1], False)
+    add_products(sources[2], False)
+    for source in sources[3:]:
+        share_arrive(source)
+
+        @pl.when(jnp.logical_not(inner))
+        def _():
+            for b in range(owned):
+                z_arrive(source, b)
+
+        add_products(source, False)
 
     def store_column(at, buffer, out):
         keep = pltpu.make_async_copy(buffer.at[core], out.at[core], column_store.at[at])
@@ -568,17 +610,20 @@
                 factor_piece(d, chip, p).wait_send()
 
     def drain(source, carry):
-        z_near(source).wait_send()
+        for b in range(owned):
+            z_near(source, b).wait_send()
 
         @pl.when(jnp.logical_and(source <= row, row + 1 < rows))
         def _():
-            z_line(source, UP).wait_send()
+            for b in range(owned):
+                z_line(source, b, UP).wait_send()
             for kind in range(KINDS):
                 line(kind, source, UP).wait_send()
 
         @pl.when(jnp.logical_and(source >= row, row > 0))
         def _():
-            z_line(source, DOWN).wait_send()
+            for b in range(owned):
+                z_line(source, b, DOWN).wait_send()
             for kind in range(KINDS):
                 line(kind, source, DOWN).wait_send()
 
@@ -661,12 +706,12 @@
                 dma((2,)),
                 dma((KINDS, rows)),
                 dma((KINDS, rows)),
-                dma((rows + KINDS, chips)),
-                dma((rows, chips)),
-                dma((2, rows)),
-                dma((rows,)),
-                dma((rows,)),
-                dma((rows,)),
+                dma((rows + KINDS, chips, 2 * chips)),
+                dma((rows, chips, 2)),
+                dma((2, rows, owned)),
+                dma((rows, owned)),
+                dma((rows, owned)),
+                dma((rows, owned)),
                 dma((2,)),
                 dma((2,)),
                 dma((2,)),

time: 120 us -> 104 us (0.87)
  Pallas kernels: 113 us -> 96.3 us
    pallas_call x1, Pallas kernels: 113 us -> 96.3 us  [body(): pl.pallas_call(functools.partial(fused_kernel, rows, cols), out_shape=[f3...]
where the time goes in v2:
time: 104 us
  Pallas kernels  96.3 us (93%)
  local copies, waits for them, and re-layouts  6.84 us (7%)
    pallas_call x1, Pallas kernels, body(): pl.pallas_call(functools.partial(fused_kernel, rows, cols), out_shape=[f3...  96.3 us
    unnamed x14, local copies, waits for them, and re-layouts  6.84 us

profile of v2, /device:TPU:24, one launch (start us, length us, event | category | flops | bytes accessed | tf_op | source)
XLA Modules:
  0.0 103.8 jit_solution(9987601969353937765)
XLA Ops:
  0.6 1.3 %copy.13.pattern = s32[8,4]{1,0:T(8,128)} copy(s32[8,4]{0,1:T(4,128)} %param.9) | data formatting | bytes 256 | tf_op args[1]
  2.0 96.3 %shard_map.119 = (f32[2,256,256]{2,1,0:T(8,128)}, f32[1,256,256]{2,1,0:T(8,128)}, f32[2,256,256]{2,1,0:T(8,128)}, f32[1,256,256]{2,1,0:T(8,128)}, f32[1,256,256]{2,1,0:T(8,128)}) custom-call(s32[8,4]{1,0:T(8,128)} %copy.13.pattern, s32[8]{0:T(128)} %parents.1, f32[256,512]{1,0:T(8,128)} %anc.1, f32[1,256,256]{2,1,0:T(8,128)} %low_one.1, ...), custom_call_target="tpu_custom_call" | custom-call | tf_op jit(solution)/shard_map/pallas_call | solution.py:670
  98.3 0.0 copy-start.3
  98.3 0.0 copy-start
  98.3 1.9 %copy.19 = f32[2,256,256]{2,1,0:T(8,128)} copy(f32[2,256,256]{2,1,0:T(8,128)} %get-tuple-element.10) | data formatting | bytes 1048576
  100.2 0.0 copy-done.3
  100.2 0.7 copy.20
  101.0 0.0 copy-done
  101.0 0.0 copy-start.2
  101.0 0.8 copy.21
  101.7 0.3 copy-done.2
  102.0 0.0 copy-start.1
  102.0 0.7 copy.22
  102.8 0.3 copy-done.1
  103.1 0.7 copy.23
Async XLA Ops:
  98.3 2.0 %copy-start.3 = (f32[1,256,256]{2,1,0:T(8,128)S(1)}, f32[1,256,256]{2,1,0:T(8,128)}, u32[]{:S(2)}) copy-start(f32[1,256,256]{2,1,0:T(8,128)} %get-tuple-element.11) | copy-start | bytes 786436
  98.3 2.7 %copy-start = (f32[2,256,256]{2,1,0:T(8,128)S(1)}, f32[2,256,256]{2,1,0:T(8,128)}, u32[]{:S(2)}) copy-start(f32[2,256,256]{2,1,0:T(8,128)} %get-tuple-element.12) | copy-start | bytes 1572868
  101.0 1.1 %copy-start.2 = (f32[1,256,256]{2,1,0:T(8,128)S(1)}, f32[1,256,256]{2,1,0:T(8,128)}, u32[]{:S(2)}) copy-start(f32[1,256,256]{2,1,0:T(8,128)} %get-tuple-element.13) | copy-start | bytes 786436
  102.0 1.0 %copy-start.1 = (f32[1,256,256]{2,1,0:T(8,128)S(1)}, f32[1,256,256]{2,1,0:T(8,128)}, u32[]{:S(2)}) copy-start(f32[1,256,256]{2,1,0:T(8,128)} %get-tuple-element.14) | copy-start | bytes 786436

commit v3 on v2

--- a/solution.py
+++ b/solution.py
@@ -38,12 +38,9 @@
     pivot_one,
     low_two,
     factor,
-    pivot_two,
     out_one,
-    out_diag,
     out_two,
-    out_cross,
-    out_second,
+    final,
     z,
     low,
     whole_factor,
@@ -51,8 +48,6 @@
     scattered_pivot,
     scattered_two,
     staged,
-    pivot_own,
-    pivot_second,
     sums,
     column,
     parent_column,
@@ -61,7 +56,6 @@
     partial,
     partials,
     reduced,
-    final,
     load_sem,
     scatter_send,
     scatter_recv,
@@ -143,12 +137,8 @@
             pivot_one.at[0, rows_of(chip)], scattered_pivot.at[core, chip], load_sem.at[owned + 2]
         ),
     ]
-    loads_last = [
-        pltpu.make_async_copy(pivot_one.at[0], pivot_own, load_sem.at[owned + 3]),
-        pltpu.make_async_copy(pivot_two.at[0], pivot_second, load_sem.at[owned + 4]),
-    ]
-    load_factor = pltpu.make_async_copy(factor.at[0], whole_factor, load_sem.at[owned + 5])
-    for copy in loads + loads_low + loads_last:
+    load_factor = pltpu.make_async_copy(factor.at[0], whole_factor, load_sem.at[owned + 3])
+    for copy in loads + loads_low:
         copy.start()
 
     @pl.when(chip == row)
@@ -171,12 +161,17 @@
         (pivot_one, scattered_pivot.at[core]),
     ]
     swapped = [scattered, scattered_pivot]
-    for op, (source, target) in enumerate(scatters):
+
+    def scatter_all(op):
+        source, target = scatters[op]
         for d in range(1, chips):
             p = turn(chip, d, chips)
             copy = scatter(op, d, source.at[0, rows_of(p)], target.at[chip], beside(p))
             copy.start()
             sent.append(copy)
+
+    scatter_all(0)
+    scatter_all(1)
 
     def z_line(source, b, direction):
         there = row + 1 if direction == UP else row - 1
@@ -237,14 +232,6 @@
             factor_recv.at[1, 0],
             beside(p),
         )
-
-    @pl.when(chip == row)
-    def _():
-        load_factor.wait()
-        for d in range(1, chips):
-            p = turn(chip, d, chips)
-            factor_first(d, p).start()
-            factor_piece(d, chip, p).start()
 
     def arrivals(op, target):
         for d in range(1, chips):
@@ -283,8 +270,9 @@
     def pieces_for(plane):
         return [scattered.at[core, plane], scattered_two.at[plane], staged.at[plane]]
 
-    for e in range(1, rows):
-        plane = turn(row, e, rows)
+    sources = [order(t) for t in range(rows)]
+    for plane in sources[1:]:
+        e = lax.rem(plane - row + rows, rows)
         for kind, source in enumerate(pieces_for(plane)):
             copy = remote(
                 source,
@@ -326,19 +314,31 @@
             beside(flip(chip, mask)),
         )
 
-    def share_arrive(source):
+    def share_wait(source, offset, half):
+        origin = flip(chip, offset)
+        if offset not in masks:
+            share(source, offset, 0, half_of(origin, half), offset, half).wait_recv()
+        elif half == 0:
+            share(source, offset, 0, rows_of(origin), offset, 0).wait_recv()
+
+    def share_relay(source, last_hop):
         for offset in offsets:
-            origin = flip(chip, offset)
-            direct = offset in masks
-            if direct:
-                share(source, offset, 0, rows_of(origin), offset, 0).wait_recv()
-            for half, tree in enumerate(trees):
-                if not direct:
-                    share(source, offset, 0, half_of(origin, half), offset, half).wait_recv()
-                came = max(n for n, mask in enumerate(tree) if offset & mask)
-                for mask in tree[came + 1 :]:
+            ways = [
+                (half, tree[max(n for n, mask in enumerate(tree) if offset & mask) + 1 :])
+                for half, tree in enumerate(trees)
+            ]
+            if last_hop != (not any(onward for _, onward in ways)):
+                continue
+            for half, onward in ways:
+                share_wait(source, offset, half)
+                for mask in onward:
                     copy = share(
-                        source, mask, 2 * offset + half, half_of(origin, half), offset ^ mask, half
+                        source,
+                        mask,
+                        2 * offset + half,
+                        half_of(flip(chip, offset), half),
+                        offset ^ mask,
+                        half,
                     )
                     copy.start()
                     sent.append(copy)
@@ -386,7 +386,15 @@
         for n, value in enumerate([first, second, third]):
             sums[n] = value if first_time else sums[n] + value
 
-    sources = [order(t) for t in range(rows)]
+    @pl.when(chip == row)
+    def _():
+        load_factor.wait()
+        for d in range(1, chips):
+            p = turn(chip, d, chips)
+            factor_first(d, p).start()
+            factor_piece(d, chip, p).start()
+
+    scatter_all(2)
     inner = jnp.logical_and(row > 0, row + 1 < rows)
 
     @pl.when(inner)
@@ -400,7 +408,10 @@
         for b in range(owned):
             z_arrive(sources[1], b)
 
-    share_arrive(row)
+    share_relay(row, False)
+    low_arrive(sources[1])
+    low_arrive(sources[2])
+    share_relay(row, True)
     @pl.when(chip != row)
     def _():
         factor_first(0, chip).wait_recv()
@@ -411,39 +422,32 @@
             def _():
                 factor_piece(d, chip, p).start()
 
+    add_products(row, True)
+    share_relay(sources[1], False)
+    for source in sources[3:]:
+        low_arrive(source)
+
+    @pl.when(inner)
+    def _():
+        for source in sources[3:]:
+            z_arrive(source, 0)
+
+    for source in sources[2:]:
+        share_relay(source, False)
+
+    @pl.when(inner)
+    def _():
+        for source in sources[3:]:
+            for b in range(1, owned):
+                z_arrive(source, b)
+
+    share_relay(sources[1], True)
+    add_products(sources[1], False)
     arrivals(2, scatters[2][1])
     swap(1).start()
     sent.append(swap(1))
-    low_arrive(sources[1])
-
-    @pl.when(jnp.logical_not(inner))
-    def _():
-        for b in range(owned):
-            z_arrive(sources[2], b)
-
-    low_arrive(sources[2])
-    add_products(row, True)
-    for source in sources[3:]:
-        low_arrive(source)
-
-    @pl.when(inner)
-    def _():
-        for source in sources[3:]:
-            z_arrive(source, 0)
-
-    share_arrive(sources[1])
-    share_arrive(sources[2])
-
-    @pl.when(inner)
-    def _():
-        for source in sources[3:]:
-            for b in range(1, owned):
-                z_arrive(source, b)
-
-    add_products(sources[1], False)
-    add_products(sources[2], False)
-    for source in sources[3:]:
-        share_arrive(source)
+    for source in sources[2:]:
+        share_relay(source, True)
 
         @pl.when(jnp.logical_not(inner))
         def _():
@@ -507,15 +511,38 @@
     )
     reduce_scatter(SECOND)
 
-    def line(kind, source, direction):
-        there = row + 1 if direction == UP else row - 1
+    def line(kind, source, distance):
+        way = UP if distance > 0 else DOWN
         return remote(
             reduced.at[source, kind],
             reduced.at[source, kind],
-            line_send.at[direction, kind, source],
+            line_send.at[way, kind, source, abs(distance) // 2],
             line_recv.at[kind, source],
-            (there, col),
-        )
+            (row + distance, col),
+        )
+
+    def onward(source, act):
+        for distance in range(1, rows, 2):
+
+            @pl.when(jnp.logical_and(source == row, row + distance < rows))
+            def _():
+                act(distance)
+
+            @pl.when(jnp.logical_and(source == row, row >= distance))
+            def _():
+                act(-distance)
+
+        @pl.when(jnp.logical_and(lax.rem(row - source + 2 * rows, 2) == 1, source < row))
+        def _():
+            @pl.when(row + 1 < rows)
+            def _():
+                act(1)
+
+        @pl.when(jnp.logical_and(lax.rem(row - source + 2 * rows, 2) == 1, source > row))
+        def _():
+            @pl.when(row > 0)
+            def _():
+                act(-1)
 
     def last(kind, source):
         d = lax.rem(source - chip + chips, chips)
@@ -537,13 +564,7 @@
             final[kind, rows_of(chip)] = reduced[source, kind]
 
     def pass_on(kind, source):
-        @pl.when(jnp.logical_and(source <= row, row + 1 < rows))
-        def _():
-            line(kind, source, UP).start()
-
-        @pl.when(jnp.logical_and(source >= row, row > 0))
-        def _():
-            line(kind, source, DOWN).start()
+        onward(source, lambda distance: line(kind, source, distance).start())
 
     for kind in range(KINDS):
         total = partial[kind, rows_of(chip)]
@@ -558,18 +579,22 @@
         pass_on(kind, row)
         hand_on(kind, row)
 
-    def spread(n, carry):
-        t, kind = 1 + n // KINDS, lax.rem(n, KINDS)
-        source = order(t)
-        line(kind, source, UP).wait_recv()
-        pass_on(kind, source)
-        hand_on(kind, source)
-        return carry
-
-    lax.fori_loop(0, (rows - 1) * KINDS, spread, 0)
-
-    for copy in loads_last:
-        copy.wait()
+    def spread(kind, source):
+        @pl.when(source != row)
+        def _():
+            line(kind, source, 1).wait_recv()
+            pass_on(kind, source)
+            hand_on(kind, source)
+
+    for source in range(1, rows - 1):
+        for kind in range(KINDS):
+            spread(kind, source)
+    near_end = jnp.where(2 * row < rows, 0, rows - 1)
+    spread(0, near_end)
+    for kind in range(1, KINDS):
+        spread(kind, near_end)
+        spread(kind - 1, rows - 1 - near_end)
+    spread(KINDS - 1, rows - 1 - near_end)
 
     def take(kind):
         for d in range(1, chips):
@@ -579,12 +604,8 @@
                 target, target, last_send.at[kind, 0], last_recv.at[kind, d], beside(p)
             ).wait_recv()
 
-    take(DIAG)
-    out_diag[0] = pivot_own[...] - final[DIAG]
-    take(CROSS)
-    out_cross[0] = final[CROSS]
-    take(SECOND)
-    out_second[0] = pivot_second[...] - final[SECOND]
+    for kind in range(KINDS):
+        take(kind)
 
     for keep, away in stores:
         keep.wait()
@@ -612,20 +633,18 @@
     def drain(source, carry):
         for b in range(owned):
             z_near(source, b).wait_send()
-
         @pl.when(jnp.logical_and(source <= row, row + 1 < rows))
         def _():
             for b in range(owned):
                 z_line(source, b, UP).wait_send()
-            for kind in range(KINDS):
-                line(kind, source, UP).wait_send()
 
         @pl.when(jnp.logical_and(source >= row, row > 0))
         def _():
             for b in range(owned):
                 z_line(source, b, DOWN).wait_send()
-            for kind in range(KINDS):
-                line(kind, source, DOWN).wait_send()
+
+        for kind in range(KINDS):
+            onward(source, lambda distance: line(kind, source, distance).wait_send())
 
         @pl.when(source != chip)
         def _():
@@ -635,6 +654,16 @@
         return carry
 
     lax.fori_loop(0, rows, drain, 0)
+
+
+def finish_kernel(
+    column_one, column_two, final, pivot_one, pivot_two, out_one, out_diag, out_two, out_cross, out_second
+):
+    out_one[...] = column_one[...]
+    out_diag[0] = pivot_one[0] - final[DIAG]
+    out_two[...] = column_two[...]
+    out_cross[0] = final[CROSS]
+    out_second[0] = pivot_two[0] - final[SECOND]
 
 
 def body(
@@ -666,9 +695,57 @@
 
     dma = pltpu.SemaphoreType.DMA
     block = (width, width)
+    column_one, column_two, final = pl.pallas_call(
+        functools.partial(fused_kernel, rows, cols),
+        out_shape=[f32(CORES, *block), f32(CORES, *block), f32(KINDS, *block)],
+        in_specs=[smem, smem] + [anywhere] * 5,
+        out_specs=[anywhere, anywhere, vmem],
+        scratch_shapes=[
+            buffer(rows, CORES, owned, *block),
+            buffer(rows, KINDS, *block),
+            buffer(*block),
+            buffer(CORES, chips, piece, width),
+            buffer(CORES, chips, piece, width),
+            buffer(chips, piece, width),
+            buffer(rows, piece, width),
+            buffer(KINDS, CORES * width, width),
+            buffer(CORES, *block),
+            buffer(CORES, *block),
+            buffer(CORES, *block),
+            buffer(CORES, *block),
+            buffer(KINDS, *block),
+            buffer(KINDS, chips, piece, width),
+            buffer(rows, KINDS, piece, width),
+            dma((owned + 4,)),
+            dma((3, chips)),
+            dma((3, chips)),
+            dma((2, chips)),
+            dma((2, chips)),
+            dma((2,)),
+            dma((2,)),
+            dma((KINDS, rows)),
+            dma((KINDS, rows)),
+            dma((rows + KINDS, chips, 2 * chips)),
+            dma((rows, chips, 2)),
+            dma((2, rows, owned)),
+            dma((rows, owned)),
+            dma((rows, owned)),
+            dma((rows, owned)),
+            dma((2,)),
+            dma((2,)),
+            dma((2,)),
+            dma((KINDS, chips)),
+            dma((KINDS, chips)),
+            dma((2, KINDS, rows, rows)),
+            dma((KINDS, rows)),
+            dma((KINDS, rows)),
+            dma((KINDS, chips)),
+        ],
+        compiler_params=pltpu.CompilerParams(collective_id=0, has_side_effects=True),
+    )(pattern_one, parents, anc_inverse, low_one, pivot_one, low_two, second_scaled_factor)
     return tuple(
         pl.pallas_call(
-            functools.partial(fused_kernel, rows, cols),
+            finish_kernel,
             out_shape=[
                 f32(CORES, *block),
                 f32(1, *block),
@@ -676,63 +753,9 @@
                 f32(1, *block),
                 f32(1, *block),
             ],
-            in_specs=[smem, smem] + [anywhere] * 6,
-            out_specs=[anywhere, vmem, anywhere, vmem, vmem],
-            scratch_shapes=[
-                buffer(rows, CORES, owned, *block),
-                buffer(rows, KINDS, *block),
-                buffer(*block),
-                buffer(CORES, chips, piece, width),
-                buffer(CORES, chips, piece, width),
-                buffer(chips, piece, width),
-                buffer(rows, piece, width),
-                buffer(*block),
-                buffer(*block),
-                buffer(KINDS, CORES * width, width),
-                buffer(CORES, *block),
-                buffer(CORES, *block),
-                buffer(CORES, *block),
-                buffer(CORES, *block),
-                buffer(KINDS, *block),
-                buffer(KINDS, chips, piece, width),
-                buffer(rows, KINDS, piece, width),
-                buffer(KINDS, *block),
-                dma((owned + 6,)),
-                dma((3, chips)),
-                dma((3, chips)),
-                dma((2, chips)),
-                dma((2, chips)),
-                dma((2,)),
-                dma((2,)),
-                dma((KINDS, rows)),
-                dma((KINDS, rows)),
-                dma((rows + KINDS, chips, 2 * chips)),
-                dma((rows, chips, 2)),
-                dma((2, rows, owned)),
-                dma((rows, owned)),
-                dma((rows, owned)),
-                dma((rows, owned)),
-                dma((2,)),
-                dma((2,)),
-                dma((2,)),
-                dma((KINDS, chips)),
-                dma((KINDS, chips)),
-                dma((2, KINDS, rows)),
-                dma((KINDS, rows)),
-                dma((KINDS, rows)),
-                dma((KINDS, chips)),
-            ],
-            compiler_params=pltpu.CompilerParams(collective_id=0, has_side_effects=True),
-        )(
-            pattern_one,
-            parents,
-            anc_inverse,
-            low_one,
-            pivot_one,
-            low_two,
-            second_scaled_factor,
-            second_pivot_inverse,
-        )
+            in_specs=[vmem] * 5,
+            out_specs=[vmem] * 5,
+        )(column_one, column_two, final, pivot_one, second_pivot_inverse)
     )
 
 

time: 104 us -> 91.1 us (0.88)
  Pallas kernels: 96.3 us -> 88.5 us
  local copies, waits for them, and re-layouts: 6.84 us -> 1.35 us
    pallas_call x1, Pallas kernels: 96.3 us -> 85.7 us  [body(): pl.pallas_call(functools.partial(fused_kernel, rows, cols), out_shape=[f3...]
    unnamed x14 -> x1, local copies, waits for them, and re-layouts: 6.84 us -> 1.35 us
    pallas_call x0 -> x1, Pallas kernels: none -> 2.83 us  [body(): pl.pallas_call(finish_kernel, out_shape=[f32(CORES, *block), f32(1, *bloc...]
where the time goes in v3:
time: 91.1 us; the launch traced here: 90.5 us
  Pallas kernels  88.5 us (97%)
  local copies, waits for them, and re-layouts  1.35 us (1%)
    pallas_call x1, Pallas kernels, body(): pl.pallas_call(functools.partial(fused_kernel, rows, cols), out_shape=[f3...  85.7 us
    pallas_call x1, Pallas kernels, body(): pl.pallas_call(finish_kernel, out_shape=[f32(CORES, *block), f32(1, *bloc...  2.83 us

profile of v3, /device:TPU:24, one launch (start us, length us, event | category | flops | bytes accessed | tf_op | source)
XLA Modules:
  0.0 90.5 jit_solution(1386806179936809264)
XLA Ops:
  0.6 1.3 %copy.13.pattern = s32[8,4]{1,0:T(8,128)} copy(s32[8,4]{0,1:T(4,128)} %param.9) | data formatting | bytes 256 | tf_op args[1]
  2.0 85.7 %shard_map.119 = (f32[2,256,256]{2,1,0:T(8,128)}, f32[2,256,256]{2,1,0:T(8,128)}, f32[3,256,256]{2,1,0:T(8,128)}) custom-call(s32[8,4]{1,0:T(8,128)} %copy.13.pattern, s32[8]{0:T(128)} %parents.1, f32[256,512]{1,0:T(8,128)} %anc.1, f32[1,256,256]{2,1,0:T(8,128)} %low_one.1, f32[1,256,256]{2,1,0:T(8,128)} %pivot_one.3, f32[1,256,256]{2,1,0:T(8,128)} %low_two.1, ...), custom_call_target="tpu_custom_call" | custom-call | tf_op jit(solution)/shard_map/pallas_call | solution.py:698
  87.7 2.8 %shard_map.120 = (f32[2,256,256]{2,1,0:T(8,128)}, f32[1,256,256]{2,1,0:T(8,128)}, f32[2,256,256]{2,1,0:T(8,128)}, f32[1,256,256]{2,1,0:T(8,128)}, f32[1,256,256]{2,1,0:T(8,128)}) custom-call(f32[2,256,256]{2,1,0:T(8,128)} %get-tuple-element.8.column_one, f32[2,256,256]{2,1,0:T(8,128)} %get-tuple-element.9.column_two, ...), custom_call_target="tpu_custom_call" | custom-call | tf_op jit(solution)/shard_map/pallas_call | solution.py:747

commit v4 on v3

--- a/solution.py
+++ b/solution.py
@@ -13,6 +13,8 @@
 LOW_ONE, LOW_TWO, LOW_PARENT = 0, 1, 2
 DIAG, CROSS, SECOND = 0, 1, 2
 KINDS = 3
+PARTS = 1
+STRIPS = [(kind, part) for kind in range(KINDS) for part in range(PARTS)]
 
 
 def split(x):
@@ -31,8 +33,8 @@
 def fused_kernel(
     rows,
     cols,
-    pattern,
-    parents,
+    pattern_table,
+    parents_table,
     anc,
     low_one,
     pivot_one,
@@ -41,6 +43,8 @@
     out_one,
     out_two,
     final,
+    pattern,
+    parents,
     z,
     low,
     whole_factor,
@@ -100,6 +104,11 @@
     def rows_of(p):
         return pl.ds(pl.multiple_of(p * piece, piece), piece)
 
+    strip = piece // PARTS
+
+    def strip_of(p, part):
+        return pl.ds(pl.multiple_of(p * piece + part * strip, strip), strip)
+
     def remote(source, target, send, recv, device):
         return pltpu.make_async_remote_copy(
             src_ref=source,
@@ -138,7 +147,11 @@
         ),
     ]
     load_factor = pltpu.make_async_copy(factor.at[0], whole_factor, load_sem.at[owned + 3])
-    for copy in loads + loads_low:
+    loads_index = [
+        pltpu.make_async_copy(pattern_table, pattern, load_sem.at[owned + 4]),
+        pltpu.make_async_copy(parents_table, parents, load_sem.at[owned + 5]),
+    ]
+    for copy in loads_index + loads + loads_low:
         copy.start()
 
     @pl.when(chip == row)
@@ -170,8 +183,6 @@
             copy.start()
             sent.append(copy)
 
-    scatter_all(0)
-    scatter_all(1)
 
     def z_line(source, b, direction):
         there = row + 1 if direction == UP else row - 1
@@ -205,15 +216,19 @@
         def _():
             z_line(source, b, DOWN).start()
 
-        z_near(source, b).start()
-
     def z_arrive(source, b):
         z_line(source, b, UP).wait_recv()
         z_pass_on(source, b)
+        z_near(source, b).start()
 
     for b, copy in enumerate(loads):
         copy.wait()
         z_pass_on(row, b)
+
+    scatter_all(0)
+    scatter_all(1)
+    for b in range(owned):
+        z_near(row, b).start()
 
     def factor_piece(d, part, p):
         return remote(
@@ -256,7 +271,7 @@
             partner,
         )
 
-    for copy in loads_low:
+    for copy in loads_low + loads_index:
         copy.wait()
     arrivals(0, scatters[0][1])
     swap(0).start()
@@ -372,18 +387,49 @@
             value = jnp.where(at == b, z[source, :, b], value)
         return value.reshape(CORES * width, width)
 
-    def add_products(source, first_time):
+    def store_column(at, buffer, out):
+        keep = pltpu.make_async_copy(buffer.at[core], out.at[core], column_store.at[at])
+        away = remote(
+            buffer.at[other], out.at[core], column_send.at[at], column_recv.at[at], partner
+        )
+        keep.start()
+        away.start()
+        return keep, away
+
+    def part_copy(kind, part, d, p, source, target):
+        n = kind * PARTS + part
+        return remote(source, target, part_send.at[n, d], part_recv.at[n, d], beside(p))
+
+    def reduce_scatter(kind):
+        for part in range(PARTS):
+            for d in range(1, chips):
+                p = turn(chip, d, chips)
+                target = partials.at[kind, chip, strip_of(0, part)]
+                copy = part_copy(kind, part, d, p, partial.at[kind, strip_of(p, part)], target)
+                copy.start()
+                sent.append(copy)
+
+    slot_one = lax.rem(pattern[chip, mine], owned)
+    slot_two = lax.rem(pattern[chip, parent], owned)
+    stores = []
+
+    def add_products(source, first_time=False, last_time=False):
         for b in range(owned):
             z_near_arrival(source, b).wait_recv()
-        at_one = lax.rem(pattern[mine, source], owned)
-        at_two = lax.rem(pattern[parent, source], owned)
-        rhs = split(low[source, LOW_ONE])
-        lhs = split(chosen(source, at_one))
-        first = dot3(lhs, rhs)
-        lhs = split(chosen(source, at_two))
+        lhs = split(chosen(source, lax.rem(pattern[source, mine], owned)))
+        first = dot3(lhs, split(low[source, LOW_ONE]))
+        sums[0] = first if first_time else sums[0] + first
+        if last_time:
+            column[...] = -sums[0].reshape(CORES, width, width)
+            partial[DIAG] = dot3(
+                split(low[chip, LOW_ONE]), split(column[slot_one]), transposed=True
+            )
+            reduce_scatter(DIAG)
+            stores.append(store_column(0, column, out_one))
+        lhs = split(chosen(source, lax.rem(pattern[source, parent], owned)))
         second = dot3(lhs, split(low[source, LOW_PARENT]))
         third = dot3(lhs, split(low[source, LOW_TWO]))
-        for n, value in enumerate([first, second, third]):
+        for n, value in enumerate([second, third], 1):
             sums[n] = value if first_time else sums[n] + value
 
     @pl.when(chip == row)
@@ -411,7 +457,23 @@
     share_relay(row, False)
     low_arrive(sources[1])
     low_arrive(sources[2])
-    share_relay(row, True)
+    share_relay(sources[1], False)
+    for source in sources[3:]:
+        low_arrive(source)
+    @pl.when(inner)
+    def _():
+        for source in sources[3:]:
+            z_arrive(source, 0)
+
+    for source in sources[2:]:
+        share_relay(source, False)
+
+    @pl.when(inner)
+    def _():
+        for source in sources[3:]:
+            for b in range(1, owned):
+                z_arrive(source, b)
+
     @pl.when(chip != row)
     def _():
         factor_first(0, chip).wait_recv()
@@ -422,27 +484,10 @@
             def _():
                 factor_piece(d, chip, p).start()
 
+    share_relay(row, True)
     add_products(row, True)
-    share_relay(sources[1], False)
-    for source in sources[3:]:
-        low_arrive(source)
-
-    @pl.when(inner)
-    def _():
-        for source in sources[3:]:
-            z_arrive(source, 0)
-
-    for source in sources[2:]:
-        share_relay(source, False)
-
-    @pl.when(inner)
-    def _():
-        for source in sources[3:]:
-            for b in range(1, owned):
-                z_arrive(source, b)
-
     share_relay(sources[1], True)
-    add_products(sources[1], False)
+    add_products(sources[1])
     arrivals(2, scatters[2][1])
     swap(1).start()
     sent.append(swap(1))
@@ -454,43 +499,13 @@
             for b in range(owned):
                 z_arrive(source, b)
 
-        add_products(source, False)
-
-    def store_column(at, buffer, out):
-        keep = pltpu.make_async_copy(buffer.at[core], out.at[core], column_store.at[at])
-        away = remote(
-            buffer.at[other], out.at[core], column_send.at[at], column_recv.at[at], partner
-        )
-        keep.start()
-        away.start()
-        return keep, away
-
-    def reduce_scatter(kind):
-        for d in range(1, chips):
-            p = turn(chip, d, chips)
-            copy = remote(
-                partial.at[kind, rows_of(p)],
-                partials.at[kind, chip],
-                part_send.at[kind, d],
-                part_recv.at[kind, d],
-                beside(p),
-            )
-            copy.start()
-            sent.append(copy)
-
-    slot_one = lax.rem(pattern[mine, chip], owned)
-    slot_two = lax.rem(pattern[parent, chip], owned)
-    column[...] = -sums[0].reshape(CORES, width, width)
-    partial[DIAG] = dot3(
-        split(low[chip, LOW_ONE]), split(column[slot_one]), transposed=True
-    )
-    stores = [store_column(0, column, out_one)]
-    reduce_scatter(DIAG)
+        add_products(source, last_time=source is sources[-1])
 
     @pl.when(chip != row)
     def _():
         for d in range(1, chips):
             factor_piece(d, turn(chip, -d, chips), partner[1]).wait_recv()
+
 
     swap_arrival(1).wait_recv()
     whole = split(whole_factor[...])
@@ -511,101 +526,92 @@
     )
     reduce_scatter(SECOND)
 
-    def line(kind, source, distance):
+    def line(kind, part, source, distance):
         way = UP if distance > 0 else DOWN
-        return remote(
-            reduced.at[source, kind],
-            reduced.at[source, kind],
-            line_send.at[way, kind, source, abs(distance) // 2],
-            line_recv.at[kind, source],
+        n = kind * PARTS + part
+        block = reduced.at[source, kind, strip_of(0, part)]
+        return remote(
+            block,
+            block,
+            line_send.at[way, n, source, abs(distance) - 1],
+            line_recv.at[n, source],
             (row + distance, col),
         )
 
-    def onward(source, act):
-        for distance in range(1, rows, 2):
-
-            @pl.when(jnp.logical_and(source == row, row + distance < rows))
+    def own_onward(kind, act):
+        for distance in range(1, rows, 1 if kind == SECOND else 2)[::-1]:
+
+            @pl.when(row + distance < rows)
             def _():
                 act(distance)
 
-            @pl.when(jnp.logical_and(source == row, row >= distance))
+            @pl.when(row >= distance)
             def _():
                 act(-distance)
 
-        @pl.when(jnp.logical_and(lax.rem(row - source + 2 * rows, 2) == 1, source < row))
-        def _():
-            @pl.when(row + 1 < rows)
-            def _():
-                act(1)
-
-        @pl.when(jnp.logical_and(lax.rem(row - source + 2 * rows, 2) == 1, source > row))
-        def _():
-            @pl.when(row > 0)
-            def _():
-                act(-1)
-
-    def last(kind, source):
+    def relay_onward(kind, source, act):
+        if kind == SECOND:
+            return
+        odd = lax.rem(row + source, 2) == 1
+
+        @pl.when(jnp.logical_and(odd, jnp.logical_and(source < row, row + 1 < rows)))
+        def _():
+            act(1)
+
+        @pl.when(jnp.logical_and(odd, jnp.logical_and(source > row, row > 0)))
+        def _():
+            act(-1)
+
+    def last(kind, part, source):
+        n = kind * PARTS + part
         d = lax.rem(source - chip + chips, chips)
         return remote(
-            reduced.at[source, kind],
-            final.at[kind, rows_of(chip)],
-            last_send.at[kind, source],
-            last_recv.at[kind, d],
+            reduced.at[source, kind, strip_of(0, part)],
+            final.at[kind, strip_of(chip, part)],
+            last_send.at[n, source],
+            last_recv.at[n, d],
             beside(source),
         )
 
-    def hand_on(kind, source):
+    def hand_on(kind, part, source):
         @pl.when(source != chip)
         def _():
-            last(kind, source).start()
+            last(kind, part, source).start()
 
         @pl.when(source == chip)
         def _():
-            final[kind, rows_of(chip)] = reduced[source, kind]
-
-    def pass_on(kind, source):
-        onward(source, lambda distance: line(kind, source, distance).start())
-
-    for kind in range(KINDS):
-        total = partial[kind, rows_of(chip)]
+            final[kind, strip_of(chip, part)] = reduced[source, kind, strip_of(0, part)]
+
+    for kind, part in STRIPS:
+        total = partial[kind, strip_of(chip, part)]
         for d in range(1, chips):
             p = turn(chip, -d, chips)
-            target = partials.at[kind, p]
-            remote(
-                target, target, part_send.at[kind, d], part_recv.at[kind, d], beside(p)
-            ).wait_recv()
-            total += partials[kind, p]
-        reduced[row, kind] = total
-        pass_on(kind, row)
-        hand_on(kind, row)
-
-    def spread(kind, source):
+            target = partials.at[kind, p, strip_of(0, part)]
+            part_copy(kind, part, d, p, target, target).wait_recv()
+            total += partials[kind, p, strip_of(0, part)]
+        reduced[row, kind, strip_of(0, part)] = total
+        own_onward(kind, lambda distance: line(kind, part, row, distance).start())
+        hand_on(kind, part, row)
+
+    def spread(kind, part, source):
         @pl.when(source != row)
         def _():
-            line(kind, source, 1).wait_recv()
-            pass_on(kind, source)
-            hand_on(kind, source)
+            line(kind, part, source, 1).wait_recv()
+            relay_onward(
+                kind, source, lambda distance: line(kind, part, source, distance).start()
+            )
+            hand_on(kind, part, source)
 
     for source in range(1, rows - 1):
-        for kind in range(KINDS):
-            spread(kind, source)
+        for kind, part in STRIPS:
+            spread(kind, part, source)
     near_end = jnp.where(2 * row < rows, 0, rows - 1)
-    spread(0, near_end)
-    for kind in range(1, KINDS):
-        spread(kind, near_end)
-        spread(kind - 1, rows - 1 - near_end)
-    spread(KINDS - 1, rows - 1 - near_end)
-
-    def take(kind):
-        for d in range(1, chips):
-            p = turn(chip, -d, chips)
-            target = final.at[kind, rows_of(p)]
-            remote(
-                target, target, last_send.at[kind, 0], last_recv.at[kind, d], beside(p)
-            ).wait_recv()
-
-    for kind in range(KINDS):
-        take(kind)
+    lag = PARTS
+    for n in range(len(STRIPS) + lag):
+        if n < len(STRIPS):
+            spread(*STRIPS[n], near_end)
+        if n >= lag:
+            spread(*STRIPS[n - lag], rows - 1 - near_end)
 
     for keep, away in stores:
         keep.wait()
@@ -643,27 +649,78 @@
             for b in range(owned):
                 z_line(source, b, DOWN).wait_send()
 
-        for kind in range(KINDS):
-            onward(source, lambda distance: line(kind, source, distance).wait_send())
+        for kind, part in STRIPS:
+            relay_onward(
+                kind, source, lambda distance: line(kind, part, source, distance).wait_send()
+            )
 
         @pl.when(source != chip)
         def _():
-            for kind in range(KINDS):
-                last(kind, source).wait_send()
+            for kind, part in STRIPS:
+                last(kind, part, source).wait_send()
 
         return carry
 
     lax.fori_loop(0, rows, drain, 0)
+    for kind, part in STRIPS:
+        own_onward(kind, lambda distance: line(kind, part, row, distance).wait_send())
+
+    for kind, part in STRIPS:
+        for d in range(1, chips):
+            p = turn(chip, -d, chips)
+            target = final.at[kind, strip_of(p, part)]
+            n = kind * PARTS + part
+            remote(
+                target, target, last_send.at[n, 0], last_recv.at[n, d], beside(p)
+            ).wait_recv()
 
 
 def finish_kernel(
-    column_one, column_two, final, pivot_one, pivot_two, out_one, out_diag, out_two, out_cross, out_second
+    column_one,
+    column_two,
+    final,
+    pivot_one,
+    pivot_two,
+    out_one,
+    out_diag,
+    out_two,
+    out_cross,
+    out_second,
+    one,
+    two,
+    sums,
+    diag,
+    second,
+    load_sem,
+    store_sem,
 ):
-    out_one[...] = column_one[...]
-    out_diag[0] = pivot_one[0] - final[DIAG]
-    out_two[...] = column_two[...]
-    out_cross[0] = final[CROSS]
-    out_second[0] = pivot_two[0] - final[SECOND]
+    sources = [column_one, column_two, final.at[CROSS], pivot_one.at[0], final.at[DIAG]]
+    sources += [pivot_two.at[0], final.at[SECOND]]
+    places = [one, two, sums.at[CROSS], diag, sums.at[DIAG], second, sums.at[SECOND]]
+    loads = [
+        pltpu.make_async_copy(source, place, load_sem.at[n])
+        for n, (source, place) in enumerate(zip(sources, places))
+    ]
+    kept = [(one, out_one), (two, out_two), (sums.at[CROSS], out_cross.at[0])]
+    kept += [(diag, out_diag.at[0]), (second, out_second.at[0])]
+    stores = [
+        pltpu.make_async_copy(place, out, store_sem.at[n]) for n, (place, out) in enumerate(kept)
+    ]
+    for copy in loads:
+        copy.start()
+    for n in range(3):
+        loads[n].wait()
+        stores[n].start()
+    loads[3].wait()
+    loads[4].wait()
+    diag[...] = diag[...] - sums[DIAG]
+    stores[3].start()
+    loads[5].wait()
+    loads[6].wait()
+    second[...] = second[...] - sums[SECOND]
+    stores[4].start()
+    for copy in stores:
+        copy.wait()
 
 
 def body(
@@ -683,7 +740,6 @@
     piece = width // chips
     if rows != chips:
         raise ValueError("mesh shape")
-    smem = pl.BlockSpec(memory_space=pltpu.SMEM)
     anywhere = pl.BlockSpec(memory_space=pl.ANY)
     vmem = pl.BlockSpec(memory_space=pltpu.VMEM)
 
@@ -698,9 +754,11 @@
     column_one, column_two, final = pl.pallas_call(
         functools.partial(fused_kernel, rows, cols),
         out_shape=[f32(CORES, *block), f32(CORES, *block), f32(KINDS, *block)],
-        in_specs=[smem, smem] + [anywhere] * 5,
+        in_specs=[anywhere] * 7,
         out_specs=[anywhere, anywhere, vmem],
         scratch_shapes=[
+            pltpu.SMEM(pattern_one.shape[::-1], jnp.int32),
+            pltpu.SMEM(parents.shape, jnp.int32),
             buffer(rows, CORES, owned, *block),
             buffer(rows, KINDS, *block),
             buffer(*block),
@@ -716,7 +774,7 @@
             buffer(KINDS, *block),
             buffer(KINDS, chips, piece, width),
             buffer(rows, KINDS, piece, width),
-            dma((owned + 4,)),
+            dma((owned + 6,)),
             dma((3, chips)),
             dma((3, chips)),
             dma((2, chips)),
@@ -734,15 +792,15 @@
             dma((2,)),
             dma((2,)),
             dma((2,)),
-            dma((KINDS, chips)),
-            dma((KINDS, chips)),
-            dma((2, KINDS, rows, rows)),
-            dma((KINDS, rows)),
-            dma((KINDS, rows)),
-            dma((KINDS, chips)),
+            dma((len(STRIPS), chips)),
+            dma((len(STRIPS), chips)),
+            dma((2, len(STRIPS), rows, rows)),
+            dma((len(STRIPS), rows)),
+            dma((len(STRIPS), rows)),
+            dma((len(STRIPS), chips)),
         ],
         compiler_params=pltpu.CompilerParams(collective_id=0, has_side_effects=True),
-    )(pattern_one, parents, anc_inverse, low_one, pivot_one, low_two, second_scaled_factor)
+    )(pattern_one.T, parents, anc_inverse, low_one, pivot_one, low_two, second_scaled_factor)
     return tuple(
         pl.pallas_call(
             finish_kernel,
@@ -753,8 +811,17 @@
                 f32(1, *block),
                 f32(1, *block),
             ],
-            in_specs=[vmem] * 5,
-            out_specs=[vmem] * 5,
+            in_specs=[anywhere] * 5,
+            out_specs=[anywhere] * 5,
+            scratch_shapes=[
+                buffer(CORES, *block),
+                buffer(CORES, *block),
+                buffer(KINDS, *block),
+                buffer(*block),
+                buffer(*block),
+                dma((7,)),
+                dma((5,)),
+            ],
         )(column_one, column_two, final, pivot_one, second_pivot_inverse)
     )
 

time: 91.1 us -> 87.7 us (0.963)
  the two profiles are of different devices: /device:TPU:24 before, /device:TPU:16 now
where the time goes in v4:
time: 87.7 us; the launch traced here: 87.5 us
  Pallas kernels  86.8 us (99%)
    pallas_call x1, Pallas kernels, body(): pl.pallas_call(functools.partial(fused_kernel, rows, cols), out_shape=[f3...  84.4 us
    pallas_call x1, Pallas kernels, body(): pl.pallas_call(finish_kernel, out_shape=[f32(CORES, *block), f32(1, *bloc...  2.42 us

profile of v4, /device:TPU:16, one launch (start us, length us, event | category | flops | bytes accessed | tf_op | source)
XLA Modules:
  0.0 87.5 jit_solution(11924093145304485788)
XLA Ops:
  0.6 84.4 %shard_map.119 = (f32[2,256,256]{2,1,0:T(8,128)}, f32[2,256,256]{2,1,0:T(8,128)}, f32[3,256,256]{2,1,0:T(8,128)}) custom-call(s32[4,8]{1,0:T(4,128)} %bitcast.1, s32[8]{0:T(128)} %parents_table.1, f32[256,512]{1,0:T(8,128)} %anc.1, f32[1,256,256]{2,1,0:T(8,128)} %low_one.1, f32[1,256,256]{2,1,0:T(8,128)} %pivot_one.3, f32[1,256,256]{2,1,0:T(8,128)} %low_two.1, ...), custom_call_target="tpu_custom_call" | custom-call | tf_op jit(solution)/shard_map/pallas_call | solution.py:754
  85.0 2.4 %shard_map.120 = (f32[2,256,256]{2,1,0:T(8,128)}, f32[1,256,256]{2,1,0:T(8,128)}, f32[2,256,256]{2,1,0:T(8,128)}, f32[1,256,256]{2,1,0:T(8,128)}, f32[1,256,256]{2,1,0:T(8,128)}) custom-call(f32[2,256,256]{2,1,0:T(8,128)} %get-tuple-element.8.column_one, f32[2,256,256]{2,1,0:T(8,128)} %get-tuple-element.9.column_two, ...), custom_call_target="tpu_custom_call" | custom-call | tf_op jit(solution)/shard_map/pallas_call | solution.py:805

commit v5 on v4

--- a/solution.py
+++ b/solution.py
@@ -84,6 +84,7 @@
     line_recv,
     last_send,
     last_recv,
+    keep_sem,
 ):
     row, col = lax.axis_index("prow"), lax.axis_index("pcol")
     chips = cols // CORES
@@ -539,7 +540,7 @@
         )
 
     def own_onward(kind, act):
-        for distance in range(1, rows, 1 if kind == SECOND else 2)[::-1]:
+        for distance in range(1, rows, 2):
 
             @pl.when(row + distance < rows)
             def _():
@@ -550,8 +551,6 @@
                 act(-distance)
 
     def relay_onward(kind, source, act):
-        if kind == SECOND:
-            return
         odd = lax.rem(row + source, 2) == 1
 
         @pl.when(jnp.logical_and(odd, jnp.logical_and(source < row, row + 1 < rows)))
@@ -573,6 +572,13 @@
             beside(source),
         )
 
+    def keep_sum(kind, part):
+        return pltpu.make_async_copy(
+            reduced.at[chip, kind, strip_of(0, part)],
+            final.at[kind, strip_of(chip, part)],
+            keep_sem.at[kind * PARTS + part],
+        )
+
     def hand_on(kind, part, source):
         @pl.when(source != chip)
         def _():
@@ -580,7 +586,7 @@
 
         @pl.when(source == chip)
         def _():
-            final[kind, strip_of(chip, part)] = reduced[source, kind, strip_of(0, part)]
+            keep_sum(kind, part).start()
 
     for kind, part in STRIPS:
         total = partial[kind, strip_of(chip, part)]
@@ -665,6 +671,8 @@
     for kind, part in STRIPS:
         own_onward(kind, lambda distance: line(kind, part, row, distance).wait_send())
 
+    for kind, part in STRIPS:
+        keep_sum(kind, part).wait()
     for kind, part in STRIPS:
         for d in range(1, chips):
             p = turn(chip, -d, chips)
@@ -741,7 +749,6 @@
     if rows != chips:
         raise ValueError("mesh shape")
     anywhere = pl.BlockSpec(memory_space=pl.ANY)
-    vmem = pl.BlockSpec(memory_space=pltpu.VMEM)
 
     def f32(*shape):
         return jax.ShapeDtypeStruct(shape, jnp.float32)
@@ -755,7 +762,7 @@
         functools.partial(fused_kernel, rows, cols),
         out_shape=[f32(CORES, *block), f32(CORES, *block), f32(KINDS, *block)],
         in_specs=[anywhere] * 7,
-        out_specs=[anywhere, anywhere, vmem],
+        out_specs=[anywhere, anywhere, anywhere],
         scratch_shapes=[
             pltpu.SMEM(pattern_one.shape[::-1], jnp.int32),
             pltpu.SMEM(parents.shape, jnp.int32),
@@ -798,6 +805,7 @@
             dma((len(STRIPS), rows)),
             dma((len(STRIPS), rows)),
             dma((len(STRIPS), chips)),
+            dma((len(STRIPS),)),
         ],
         compiler_params=pltpu.CompilerParams(collective_id=0, has_side_effects=True),
     )(pattern_one.T, parents, anc_inverse, low_one, pivot_one, low_two, second_scaled_factor)

time: 87.7 us -> 84.8 us (0.967)
  the two profiles are of different devices: /device:TPU:16 before, /device:TPU:24 now
where the time goes in v5:
time: 84.8 us; the launch traced here: 84.6 us
  Pallas kernels  83.9 us (99%)
    pallas_call x1, Pallas kernels, body(): pl.pallas_call(functools.partial(fused_kernel, rows, cols), out_shape=[f3...  81.5 us
    pallas_call x1, Pallas kernels, body(): pl.pallas_call(finish_kernel, out_shape=[f32(CORES, *block), f32(1, *bloc...  2.42 us

profile of v5, /device:TPU:24, one launch (start us, length us, event | category | flops | bytes accessed | tf_op | source)
XLA Modules:
  0.0 84.6 jit_solution(6736731191036311413)
XLA Ops:
  0.6 81.5 %shard_map.119 = (f32[2,256,256]{2,1,0:T(8,128)}, f32[2,256,256]{2,1,0:T(8,128)}, f32[3,256,256]{2,1,0:T(8,128)}) custom-call(s32[4,8]{1,0:T(4,128)} %bitcast.1, s32[8]{0:T(128)} %parents_table.1, f32[256,512]{1,0:T(8,128)} %anc.1, f32[1,256,256]{2,1,0:T(8,128)} %low_one.1, f32[1,256,256]{2,1,0:T(8,128)} %pivot_one.3, f32[1,256,256]{2,1,0:T(8,128)} %low_two.1, ...), custom_call_target="tpu_custom_call" | custom-call | tf_op jit(solution)/shard_map/pallas_call | solution.py:761
  82.2 2.4 %shard_map.120 = (f32[2,256,256]{2,1,0:T(8,128)}, f32[1,256,256]{2,1,0:T(8,128)}, f32[2,256,256]{2,1,0:T(8,128)}, f32[1,256,256]{2,1,0:T(8,128)}, f32[1,256,256]{2,1,0:T(8,128)}) custom-call(f32[2,256,256]{2,1,0:T(8,128)} %get-tuple-element.8.column_one, f32[2,256,256]{2,1,0:T(8,128)} %get-tuple-element.9.column_two, ...), custom_call_target="tpu_custom_call" | custom-call | tf_op jit(solution)/shard_map/pallas_call | solution.py:813

commit v6 on v5

--- a/solution.py
+++ b/solution.py
@@ -40,6 +40,7 @@
     pivot_one,
     low_two,
     factor,
+    pivot_two,
     out_one,
     out_two,
     final,
@@ -48,6 +49,8 @@
     z,
     low,
     whole_factor,
+    pivot_own,
+    pivot_second,
     scattered,
     scattered_pivot,
     scattered_two,
@@ -147,12 +150,16 @@
             pivot_one.at[0, rows_of(chip)], scattered_pivot.at[core, chip], load_sem.at[owned + 2]
         ),
     ]
+    loads_pivot = [
+        pltpu.make_async_copy(pivot_one.at[0], pivot_own, load_sem.at[owned + 6]),
+        pltpu.make_async_copy(pivot_two.at[0], pivot_second, load_sem.at[owned + 7]),
+    ]
     load_factor = pltpu.make_async_copy(factor.at[0], whole_factor, load_sem.at[owned + 3])
     loads_index = [
         pltpu.make_async_copy(pattern_table, pattern, load_sem.at[owned + 4]),
         pltpu.make_async_copy(parents_table, parents, load_sem.at[owned + 5]),
     ]
-    for copy in loads_index + loads + loads_low:
+    for copy in loads_index + loads + loads_low + loads_pivot:
         copy.start()
 
     @pl.when(chip == row)
@@ -671,9 +678,10 @@
     for kind, part in STRIPS:
         own_onward(kind, lambda distance: line(kind, part, row, distance).wait_send())
 
+    for copy in loads_pivot:
+        copy.wait()
     for kind, part in STRIPS:
         keep_sum(kind, part).wait()
-    for kind, part in STRIPS:
         for d in range(1, chips):
             p = turn(chip, -d, chips)
             target = final.at[kind, strip_of(p, part)]
@@ -681,52 +689,21 @@
             remote(
                 target, target, last_send.at[n, 0], last_recv.at[n, d], beside(p)
             ).wait_recv()
+        if part == PARTS - 1 and kind in (DIAG, SECOND):
+            pivot = pivot_own if kind == DIAG else pivot_second
+            final[kind] = pivot[...] - final[kind]
 
 
 def finish_kernel(
-    column_one,
-    column_two,
-    final,
-    pivot_one,
-    pivot_two,
-    out_one,
-    out_diag,
-    out_two,
-    out_cross,
-    out_second,
-    one,
-    two,
-    sums,
-    diag,
-    second,
-    load_sem,
-    store_sem,
+    column_one, column_two, final, out_one, out_diag, out_two, out_cross, out_second, store_sem
 ):
-    sources = [column_one, column_two, final.at[CROSS], pivot_one.at[0], final.at[DIAG]]
-    sources += [pivot_two.at[0], final.at[SECOND]]
-    places = [one, two, sums.at[CROSS], diag, sums.at[DIAG], second, sums.at[SECOND]]
-    loads = [
-        pltpu.make_async_copy(source, place, load_sem.at[n])
-        for n, (source, place) in enumerate(zip(sources, places))
-    ]
-    kept = [(one, out_one), (two, out_two), (sums.at[CROSS], out_cross.at[0])]
-    kept += [(diag, out_diag.at[0]), (second, out_second.at[0])]
+    kept = [(column_one, out_one), (column_two, out_two), (final.at[DIAG], out_diag.at[0])]
+    kept += [(final.at[CROSS], out_cross.at[0]), (final.at[SECOND], out_second.at[0])]
     stores = [
         pltpu.make_async_copy(place, out, store_sem.at[n]) for n, (place, out) in enumerate(kept)
     ]
-    for copy in loads:
+    for copy in stores:
         copy.start()
-    for n in range(3):
-        loads[n].wait()
-        stores[n].start()
-    loads[3].wait()
-    loads[4].wait()
-    diag[...] = diag[...] - sums[DIAG]
-    stores[3].start()
-    loads[5].wait()
-    loads[6].wait()
-    second[...] = second[...] - sums[SECOND]
-    stores[4].start()
     for copy in stores:
         copy.wait()
 
@@ -749,6 +726,7 @@
     if rows != chips:
         raise ValueError("mesh shape")
     anywhere = pl.BlockSpec(memory_space=pl.ANY)
+    vmem = pl.BlockSpec(memory_space=pltpu.VMEM)
 
     def f32(*shape):
         return jax.ShapeDtypeStruct(shape, jnp.float32)
@@ -760,14 +738,16 @@
     block = (width, width)
     column_one, column_two, final = pl.pallas_call(
         functools.partial(fused_kernel, rows, cols),
-        out_shape=[f32(CORES, *block), f32(CORES, *block), f32(KINDS, *block)],
-        in_specs=[anywhere] * 7,
-        out_specs=[anywhere, anywhere, anywhere],
+        out_shape=[buffer(CORES, *block), buffer(CORES, *block), buffer(KINDS, *block)],
+        in_specs=[anywhere] * 8,
+        out_specs=[vmem, vmem, vmem],
         scratch_shapes=[
             pltpu.SMEM(pattern_one.shape[::-1], jnp.int32),
             pltpu.SMEM(parents.shape, jnp.int32),
             buffer(rows, CORES, owned, *block),
             buffer(rows, KINDS, *block),
+            buffer(*block),
+            buffer(*block),
             buffer(*block),
             buffer(CORES, chips, piece, width),
             buffer(CORES, chips, piece, width),
@@ -781,7 +761,7 @@
             buffer(KINDS, *block),
             buffer(KINDS, chips, piece, width),
             buffer(rows, KINDS, piece, width),
-            dma((owned + 6,)),
+            dma((owned + 8,)),
             dma((3, chips)),
             dma((3, chips)),
             dma((2, chips)),
@@ -808,7 +788,7 @@
             dma((len(STRIPS),)),
         ],
         compiler_params=pltpu.CompilerParams(collective_id=0, has_side_effects=True),
-    )(pattern_one.T, parents, anc_inverse, low_one, pivot_one, low_two, second_scaled_factor)
+    )(pattern_one.T, parents, anc_inverse, low_one, pivot_one, low_two, second_scaled_factor, second_pivot_inverse)
     return tuple(
         pl.pallas_call(
             finish_kernel,
@@ -819,18 +799,15 @@
                 f32(1, *block),
                 f32(1, *block),
             ],
-            in_specs=[anywhere] * 5,
+            in_specs=[vmem] * 3,
             out_specs=[anywhere] * 5,
-            scratch_shapes=[
-                buffer(CORES, *block),
-                buffer(CORES, *block),
-                buffer(KINDS, *block),
-                buffer(*block),
-                buffer(*block),
-                dma((7,)),
-                dma((5,)),
-            ],
-        )(column_one, column_two, final, pivot_one, second_pivot_inverse)
+            scratch_shapes=[dma((5,))],
+        )(
+            *[
+                pltpu.with_memory_space_constraint(x, pltpu.VMEM)
+                for x in (column_one, column_two, final)
+            ]
+        )
     )
 
 

time: 84.8 us -> 83.6 us (0.986)
  Pallas kernels: 83.9 us -> 82.8 us
    pallas_call x1, Pallas kernels: 2.42 us -> 1.27 us  [body(): pl.pallas_call(finish_kernel, out_shape=[f32(CORES, *block), f32(1, *bloc...]
where the time goes in v6:
time: 83.6 us; the launch traced here: 83.4 us
  Pallas kernels  82.8 us (99%)
    pallas_call x1, Pallas kernels, body(): pl.pallas_call(functools.partial(fused_kernel, rows, cols), out_shape=[bu...  81.5 us

profile of v6, /device:TPU:24, one launch (start us, length us, event | category | flops | bytes accessed | tf_op | source)
XLA Modules:
  0.0 83.4 jit_solution(15195232339847365398)
XLA Ops:
  0.6 81.5 %shard_map.119 = (f32[2,256,256]{2,1,0:T(8,128)S(1)}, f32[2,256,256]{2,1,0:T(8,128)S(1)}, f32[3,256,256]{2,1,0:T(8,128)S(1)}) custom-call(s32[4,8]{1,0:T(4,128)} %bitcast.1, s32[8]{0:T(128)} %parents_table.1, f32[256,512]{1,0:T(8,128)} %anc.1, f32[1,256,256]{2,1,0:T(8,128)} %low_one.1, f32[1,256,256]{2,1,0:T(8,128)} %pivot_one.1, f32[1,256,256]{2,1,0:T(8,128)} %low_two.1, ...), custom_call_target="tpu_custom_call" | custom-call | tf_op jit(solution)/shard_map/pallas_call | solution.py:739
  82.2 1.3 %shard_map.120 = (f32[2,256,256]{2,1,0:T(8,128)}, f32[1,256,256]{2,1,0:T(8,128)}, f32[2,256,256]{2,1,0:T(8,128)}, f32[1,256,256]{2,1,0:T(8,128)}, f32[1,256,256]{2,1,0:T(8,128)}) custom-call(f32[2,256,256]{2,1,0:T(8,128)S(1)} %get-tuple-element.8.column_one, f32[2,256,256]{2,1,0:T(8,128)S(1)} %get-tuple-element.9.column_two, ...), custom_call_target="tpu_custom_call" | custom-call | tf_op jit(solution)/shard_map/pallas_call | solution.py:793

commit v7 on v6

--- a/solution.py
+++ b/solution.py
@@ -281,6 +281,7 @@
 
     for copy in loads_low + loads_index:
         copy.wait()
+    scatter_all(2)
     arrivals(0, scatters[0][1])
     swap(0).start()
     sent.append(swap(0))
@@ -448,7 +449,6 @@
             factor_first(d, p).start()
             factor_piece(d, chip, p).start()
 
-    scatter_all(2)
     inner = jnp.logical_and(row > 0, row + 1 < rows)
 
     @pl.when(inner)
@@ -492,13 +492,13 @@
             def _():
                 factor_piece(d, chip, p).start()
 
+    arrivals(2, scatters[2][1])
+    swap(1).start()
+    sent.append(swap(1))
     share_relay(row, True)
     add_products(row, True)
     share_relay(sources[1], True)
     add_products(sources[1])
-    arrivals(2, scatters[2][1])
-    swap(1).start()
-    sent.append(swap(1))
     for source in sources[2:]:
         share_relay(source, True)
 

time: 83.6 us -> 83.6 us (level)
  no operation moved by 1% of the time
where the time goes in v7:
time: 83.6 us; the launch traced here: 82.9 us
  Pallas kernels  82.3 us (98%)
    pallas_call x1, Pallas kernels, body(): pl.pallas_call(functools.partial(fused_kernel, rows, cols), out_shape=[bu...  81 us

profile of v7, /device:TPU:24, one launch (start us, length us, event | category | flops | bytes accessed | tf_op | source)
XLA Modules:
  0.0 82.9 jit_solution(12583079297548553805)
XLA Ops:
  0.6 81.0 %shard_map.119 = (f32[2,256,256]{2,1,0:T(8,128)S(1)}, f32[2,256,256]{2,1,0:T(8,128)S(1)}, f32[3,256,256]{2,1,0:T(8,128)S(1)}) custom-call(s32[4,8]{1,0:T(4,128)} %bitcast.1, s32[8]{0:T(128)} %parents_table.1, f32[256,512]{1,0:T(8,128)} %anc.1, f32[1,256,256]{2,1,0:T(8,128)} %low_one.1, f32[1,256,256]{2,1,0:T(8,128)} %pivot_one.1, f32[1,256,256]{2,1,0:T(8,128)} %low_two.1, ...), custom_call_target="tpu_custom_call" | custom-call | tf_op jit(solution)/shard_map/pallas_call | solution.py:739
  81.7 1.3 %shard_map.120 = (f32[2,256,256]{2,1,0:T(8,128)}, f32[1,256,256]{2,1,0:T(8,128)}, f32[2,256,256]{2,1,0:T(8,128)}, f32[1,256,256]{2,1,0:T(8,128)}, f32[1,256,256]{2,1,0:T(8,128)}) custom-call(f32[2,256,256]{2,1,0:T(8,128)S(1)} %get-tuple-element.8.column_one, f32[2,256,256]{2,1,0:T(8,128)S(1)} %get-tuple-element.9.column_two, ...), custom_call_target="tpu_custom_call" | custom-call | tf_op jit(solution)/shard_map/pallas_call | solution.py:793

commit v8 on v7

--- a/solution.py
+++ b/solution.py
@@ -520,19 +520,19 @@
     parent_column[...] = -sums[1].reshape(CORES, width, width)
     scaled = dot3(split(-sums[1]), whole)
     product[...] = scaled.reshape(CORES, width, width)
-    column_two[...] = -(scaled + sums[2]).reshape(CORES, width, width)
     two_split = split(low[chip, LOW_TWO])
     cross = dot3(split(low[chip, LOW_PARENT]), split(product[slot_two]), transposed=True)
     cross = cross - dot3(split(parent_column[slot_two]), two_split, transposed=True)
     partial[CROSS] = cross
     pivot_rows = scattered_pivot[lax.rem(parent, CORES), parent // CORES]
     partial[CROSS, rows_of(chip)] -= dot3(split(pivot_rows), whole)
-    stores.append(store_column(1, column_two, out_two))
     reduce_scatter(CROSS)
+    column_two[...] = -(scaled + sums[2]).reshape(CORES, width, width)
     partial[SECOND] = dot3(two_split, split(column_two[slot_two]), transposed=True) + dot3(
         whole, split(partial[CROSS]), transposed=True
     )
     reduce_scatter(SECOND)
+    stores.append(store_column(1, column_two, out_two))
 
     def line(kind, part, source, distance):
         way = UP if distance > 0 else DOWN

time: 83.6 us -> 83.6 us (level)
  no operation moved by 1% of the time
where the time goes in v8:
time: 83.6 us; the launch traced here: 83.1 us
  Pallas kernels  82.4 us (99%)
    pallas_call x1, Pallas kernels, body(): pl.pallas_call(functools.partial(fused_kernel, rows, cols), out_shape=[bu...  81.1 us

profile of v8, /device:TPU:24, one launch (start us, length us, event | category | flops | bytes accessed | tf_op | source)
XLA Modules:
  0.0 83.1 jit_solution(7610035764638149487)
XLA Ops:
  0.6 81.1 %shard_map.119 = (f32[2,256,256]{2,1,0:T(8,128)S(1)}, f32[2,256,256]{2,1,0:T(8,128)S(1)}, f32[3,256,256]{2,1,0:T(8,128)S(1)}) custom-call(s32[4,8]{1,0:T(4,128)} %bitcast.1, s32[8]{0:T(128)} %parents_table.1, f32[256,512]{1,0:T(8,128)} %anc.1, f32[1,256,256]{2,1,0:T(8,128)} %low_one.1, f32[1,256,256]{2,1,0:T(8,128)} %pivot_one.1, f32[1,256,256]{2,1,0:T(8,128)} %low_two.1, ...), custom_call_target="tpu_custom_call" | custom-call | tf_op jit(solution)/shard_map/pallas_call | solution.py:739
  81.8 1.3 %shard_map.120 = (f32[2,256,256]{2,1,0:T(8,128)}, f32[1,256,256]{2,1,0:T(8,128)}, f32[2,256,256]{2,1,0:T(8,128)}, f32[1,256,256]{2,1,0:T(8,128)}, f32[1,256,256]{2,1,0:T(8,128)}) custom-call(f32[2,256,256]{2,1,0:T(8,128)S(1)} %get-tuple-element.8.column_one, f32[2,256,256]{2,1,0:T(8,128)S(1)} %get-tuple-element.9.column_two, ...), custom_call_target="tpu_custom_call" | custom-call | tf_op jit(solution)/shard_map/pallas_call | solution.py:793
